TPU v7x, 256 devices: a whole 4x4x8 slice. The times are simulated.
256 devices in a mesh: pts: 2 (over core), geo: 128 (over z, y, x).
Axes of the slice: x: 4, y: 4, z: 8, core: 2. Of those that a mesh axis runs over, the one named last changes fastest.
Arguments:
- points: bfloat16 [128, 1024, 256], P('geo', 'pts'), may hold values from -6 to 6
- result_grad: bfloat16 [128, 1024, 256], P('geo', 'pts'), may hold values from -6 to 6
- lists_one: int32 [128, 8, 4], P('geo', 'pts'), may hold values from 0 to 7, all different within a row
- lists_two: int32 [128, 8, 4], P('geo', 'pts'), may hold values from 0 to 7, all different within a row
- rotation: int32 [128, 1024], P('geo', 'pts'), may hold values from 0 to 1023, each once within a row
- gain_one: bfloat16 [256], replicated, may hold values from 0.25 to 1.75
- qkv_one: bfloat16 [256, 768], replicated, may hold values from -0.375 to 0.375
- out_one: bfloat16 [256, 256], replicated, may hold values from -0.375 to 0.375
- gain_two: bfloat16 [256], replicated, may hold values from 0.25 to 1.75
- qkv_two: bfloat16 [256, 768], replicated, may hold values from -0.375 to 0.375
- out_two: bfloat16 [256, 256], replicated, may hold values from -0.375 to 0.375
Outputs:
- result: bfloat16 [128, 1024, 256], P('geo', 'pts')
- points_grad: bfloat16 [128, 1024, 256], P('geo', 'pts')
- gain_one_grad: float32 [256], replicated
- qkv_one_grad: float32 [256, 768], replicated
- out_one_grad: float32 [256, 256], replicated
- gain_two_grad: float32 [256], replicated
- qkv_two_grad: float32 [256, 768], replicated
- out_two_grad: float32 [256, 256], replicated
Inputs may be any that keep to these rules, and one draw needn't show every extreme that they name: `lists_one`: each ball lists 4 different balls of its geometry. `lists_two`: each ball lists 4 different balls of its geometry. `rotation`: each geometry's row is a permutation of its points.
All inputs are finite; a program needn't handle non-finite values.
Results may differ from a plain program's by a relative error of at most 0.012.
Values may be sent and summed in bfloat16 or wider, within the bound.
A program may use at most 64 MiB of HBM per device.

v0:
```python
import jax
import jax.numpy as jnp
from jax import lax
from jax.sharding import Mesh
from jax.sharding import PartitionSpec as P

HEADS = 4
BALL = 128
LISTED = 4
GEO = ("geo_0", "geo_1", "geo_2")


HIGH = lax.Precision.HIGHEST
EPSILON = 1e-06


def from_everyone(array, axis):
    copies = jnp.broadcast_to(array, (lax.axis_size(axis), *array.shape))
    return lax.all_to_all(copies, axis, split_axis=0, concat_axis=0, tiled=True)


def joined_along(pieces, dim):
    lengths = list(pieces.shape[1:])
    lengths[dim] *= pieces.shape[0]
    return jnp.moveaxis(pieces, 0, dim).reshape(lengths)


def collect(array, axis, dim):
    pieces = from_everyone(array, axis)
    return joined_along(pieces, dim)


def cut_along(array, dim, length):
    before, after = (array.shape[:dim], array.shape[dim + 1 :])
    return jnp.moveaxis(array.reshape(*before, length, -1, *after), dim, 0)


def summed_on_arrival(array, axis, dim):
    length = lax.axis_size(axis)
    pieces = lax.all_to_all(cut_along(array, dim, length), axis, 0, 0, tiled=True)
    return jnp.sum(pieces.astype(jnp.float32), axis=0)


def sent_and_summed(array, axis, dim):
    length = lax.axis_size(axis)
    pieces = lax.all_to_all(cut_along(array, dim, length), axis, 0, 0, tiled=True)
    return jnp.sum(pieces, axis=0)


def sum_in_two_steps(array, axes, dim):
    far, near = axes
    pieces = cut_along(array, dim, lax.axis_size(far))
    nearer = sent_and_summed(pieces, near, dim + 1)
    arrived = lax.all_to_all(nearer, far, split_axis=0, concat_axis=0, tiled=True)
    return arrived.sum(axis=0)


def padded_to(lines, length):
    spare = -lines.shape[0] % length
    if not spare:
        return lines
    return jnp.concatenate([lines, jnp.zeros((spare, *lines.shape[1:]), lines.dtype)])


def gather_axes(array, axes, dim):
    far, near = axes
    pieces = from_everyone(from_everyone(array, far), near)
    return joined_along(pieces.swapaxes(0, 1).reshape(-1, *array.shape), dim)


def total_of(array, axes):
    lines = array.reshape(-1)
    own = sum_in_two_steps(
        padded_to(lines, lax.axis_size(axes[0]) * lax.axis_size(axes[1])), axes, 0
    )
    whole = gather_axes(own, axes, 0)
    return whole[: len(lines)].reshape(array.shape)


def ball_softmax(query_ball, keys):
    head_dim = query_ball.shape[-1]
    products = jnp.einsum("qhd,khd->hqk", query_ball, keys, preferred_element_type=jnp.float32)
    scores = products * head_dim ** (-0.5)
    topmost = jnp.max(scores, axis=-1, keepdims=True)
    exponent = jnp.exp(scores - topmost)
    return exponent / jnp.sum(exponent, axis=-1, keepdims=True)


def ball_forward(query_ball, keys, values):
    weights = ball_softmax(query_ball, keys).astype(jnp.bfloat16)
    mixed = jnp.einsum("hqk,khd->qhd", weights, values, preferred_element_type=jnp.float32)
    return mixed.astype(jnp.bfloat16)


def ball_backward(query_ball, keys, values, grad_ball):
    head_dim = query_ball.shape[-1]
    attention = ball_softmax(query_ball, keys)
    weights = attention.astype(jnp.bfloat16)
    weights_grad = jnp.einsum("qhd,khd->hqk", grad_ball, values, preferred_element_type=jnp.float32)
    weights_grad = lax.optimization_barrier(weights_grad.astype(jnp.bfloat16)).astype(jnp.float32)
    values_grad = jnp.einsum("hqk,qhd->khd", weights, grad_ball, preferred_element_type=jnp.float32)
    inner = jnp.sum(attention * weights_grad, axis=-1, keepdims=True)
    scores_grad = (attention * (weights_grad - inner) * head_dim ** (-0.5)).astype(jnp.bfloat16)
    query_grad = jnp.einsum("hqk,khd->qhd", scores_grad, keys, preferred_element_type=jnp.float32)
    keys_grad = jnp.einsum(
        "hqk,qhd->khd", scores_grad, query_ball, preferred_element_type=jnp.float32
    )
    return (query_grad, keys_grad, values_grad)


def attend_forward(queries, gathered, listed):
    rows_count, width = queries.shape
    head_dim = width // HEADS
    blocks = gathered.reshape(gathered.shape[0] // BALL, BALL, 2 * width)
    query_blocks = queries.reshape(rows_count // BALL, BALL, HEADS, head_dim)

    def one_ball(packed):
        query_ball, chosen_ids = packed
        chosen = jnp.take(blocks, chosen_ids, axis=0).reshape(LISTED * BALL, 2, HEADS, head_dim)
        return ball_forward(query_ball, chosen[:, 0], chosen[:, 1]).reshape(BALL, width)

    return lax.map(one_ball, (query_blocks, listed)).reshape(rows_count, width)


def attend_backward(queries, gathered, listed, mixed_grad):
    rows_count, width = queries.shape
    head_dim = width // HEADS
    total_balls = gathered.shape[0] // BALL
    blocks = gathered.reshape(total_balls, BALL, 2 * width)
    query_blocks = queries.reshape(rows_count // BALL, BALL, HEADS, head_dim)
    grad_blocks = mixed_grad.reshape(rows_count // BALL, BALL, HEADS, head_dim)

    def one_ball(buffer, packed):
        query_ball, grad_ball, chosen_ids = packed
        chosen = jnp.take(blocks, chosen_ids, axis=0).reshape(LISTED * BALL, 2, HEADS, head_dim)
        query_grad, keys_grad, values_grad = ball_backward(
            query_ball, chosen[:, 0], chosen[:, 1], grad_ball
        )
        stacked = jnp.stack([keys_grad, values_grad], axis=1).reshape(LISTED, BALL, 2 * width)
        buffer = buffer.at[chosen_ids].add(stacked)
        return (buffer, query_grad.reshape(BALL, width))

    empty = jnp.zeros((total_balls, BALL, 2 * width), jnp.float32)
    buffer, query_grads = lax.scan(one_ball, empty, (query_blocks, grad_blocks, listed))
    return (query_grads.reshape(rows_count, width), buffer.reshape(total_balls * BALL, 2 * width))


def layer_forward(rows, listed, gain, weight_in, weight_out):
    width = rows.shape[-1]
    inputs = rows.astype(jnp.float32)
    meansq = jnp.mean(inputs * inputs, axis=-1, keepdims=True)
    factor = lax.rsqrt(meansq + EPSILON)
    normed = (inputs * factor * gain.astype(jnp.float32)).astype(jnp.bfloat16)
    queries = jnp.dot(normed, weight_in[:, :width], preferred_element_type=jnp.float32).astype(
        jnp.bfloat16
    )
    all_normed = collect(normed, "pts", 0)
    gathered = jnp.dot(all_normed, weight_in[:, width:], preferred_element_type=jnp.float32).astype(
        jnp.bfloat16
    )
    mixed = attend_forward(queries, gathered, listed)
    output = (inputs + jnp.dot(mixed, weight_out, preferred_element_type=jnp.float32)).astype(
        jnp.bfloat16
    )
    saved = (
        inputs,
        factor,
        normed,
        all_normed,
        queries,
        gathered,
        mixed,
        listed,
        gain,
        weight_in,
        weight_out,
    )
    return (output, saved)


def layer_backward(grad_out, saved):
    (
        inputs,
        factor,
        normed,
        all_normed,
        queries,
        gathered,
        mixed,
        listed,
        gain,
        weight_in,
        weight_out,
    ) = saved
    rows_count, width = grad_out.shape
    out_grad = jnp.einsum("nd,ne->de", mixed, grad_out, preferred_element_type=jnp.float32)
    mixed_grad = jnp.einsum(
        "ne,de->nd", grad_out, weight_out, preferred_element_type=jnp.float32
    ).astype(jnp.bfloat16)
    query_grad, partial_kv = attend_backward(queries, gathered, listed, mixed_grad)
    query_grad = query_grad.astype(jnp.bfloat16)
    query_weight_grad = jnp.einsum(
        "nd,ne->de", normed, query_grad, preferred_element_type=jnp.float32
    )
    normed_grad = jnp.einsum(
        "ne,de->nd", query_grad, weight_in[:, :width], preferred_element_type=jnp.float32
    )
    kv_weight = weight_in[:, width:].astype(jnp.float32)
    kv_weight_grad = jnp.einsum(
        "nd,nc->dc", all_normed.astype(jnp.float32), partial_kv, precision=HIGH
    )
    normed_grad = normed_grad + summed_on_arrival(
        jnp.einsum("nc,dc->nd", partial_kv, kv_weight, precision=HIGH).astype(jnp.bfloat16),
        "pts",
        0,
    )
    normed_grad = lax.optimization_barrier(normed_grad.astype(jnp.bfloat16)).astype(jnp.float32)
    scaled = normed_grad * gain.astype(jnp.float32)
    gain_grad = jnp.sum(normed_grad * (inputs * factor), axis=0)
    inner = jnp.mean(scaled * inputs, axis=-1, keepdims=True)
    inputs_grad = factor * scaled - inputs * (factor * factor * factor) * inner
    rows_grad = (grad_out.astype(jnp.float32) + inputs_grad).astype(jnp.bfloat16)
    weight_in_grad = jnp.concatenate([query_weight_grad, kv_weight_grad], axis=1)
    return (rows_grad, (gain_grad, weight_in_grad, out_grad))


def local(
    points,
    result_grad,
    lists_one,
    lists_two,
    rotation,
    gain_one,
    qkv_one,
    out_one,
    gain_two,
    qkv_two,
    out_two,
):
    rows_count, width = (points.shape[1], points.shape[2])
    hidden, first_saved = layer_forward(points[0], lists_one[0], gain_one, qkv_one, out_one)
    geometry_rows = collect(hidden, "pts", 0)
    moved = jnp.take(geometry_rows, rotation[0], axis=0)
    result, second_saved = layer_forward(moved, lists_two[0], gain_two, qkv_two, out_two)
    moved_grad, grads_two = layer_backward(result_grad[0], second_saved)
    buffer = jnp.zeros((geometry_rows.shape[0], width), jnp.float32)
    buffer = buffer.at[rotation[0]].set(moved_grad.astype(jnp.float32))
    hidden_grad = summed_on_arrival(buffer.astype(jnp.bfloat16), "pts", 0).astype(jnp.bfloat16)
    points_grad, grads_one = layer_backward(hidden_grad, first_saved)
    pieces = list(grads_one) + list(grads_two)
    flat = jnp.concatenate([item.reshape(-1) for item in pieces])
    summed = total_of(flat, (("pts", "geo_0", "geo_1"), "geo_2"))
    outputs = []
    offset = 0
    for item in pieces:
        length = item.size
        outputs.append(summed[offset : offset + length].reshape(item.shape))
        offset = offset + length
    return (
        result[None],
        points_grad[None],
        outputs[0],
        outputs[1],
        outputs[2],
        outputs[3],
        outputs[4],
        outputs[5],
    )


def solution(mesh):
    torus = Mesh(
        mesh.devices.reshape(mesh.shape["pts"], 8, 4, 4), ("pts", "geo_0", "geo_1", "geo_2")
    )
    placed = (
        P(GEO, "pts", None),
        P(GEO, "pts", None),
        P(GEO, "pts", None),
        P(GEO, "pts", None),
        P(GEO, "pts"),
        P(),
        P(),
        P(),
        P(),
        P(),
        P(),
    )
    return jax.shard_map(
        local,
        mesh=torus,
        in_specs=placed,
        out_specs=(P(GEO, "pts", None), P(GEO, "pts", None), P(), P(), P(), P(), P(), P()),
        check_vma=False,
    )
```

profile of v0, /device:TPU:1, one launch (start us, length us, event | category | flops | bytes accessed | tf_op | source)
XLA Modules:
  0.0 436.3 jit_solution(8001481765100030951)
XLA Ops:
  5.0 6.7 %all-to-all-start = ((bf16[2,512,256]{2,1,0:T(8,128)(2,1)}), bf16[2,512,256]{2,1,0:T(8,128)(2,1)S(1)}, u32[]{:S(2)}, u32[]{:S(2)}) async-start(bf16[2,512,256]{2,1,0:T(8,128)(2,1)} %broadcast_in_dim.79), calls=%async_computation | async-start | bytes 1048576 | tf_op jit(solution)/shard_map/all_to_all | solution.py:19
  15.0 18.7 %while.44 = (s32[]{:T(128)}, bf16[4,128,256]{2,1,0:T(8,128)(2,1)S(1)}, s32[4,4]{1,0:T(4,128)S(1)}, bf16[8,128,512]{2,1,0:T(8,128)(2,1)}, bf16[4,128,4,64]{1,3,2,0:T(8,128)(2,1)S(1)}, /*index=5*/s32[]{:T(128)}) while((s32[]{:T(128)}, bf16[4,128,256]{2,1,0:T(8,128)(2,1)S(1)}, s32[4,4]{1,0:T(4,128)S(1)}, bf16[8,128,512]{2,1,0:T(8,128)(2,1)}, ...), condition=%wide.region_4.6_spmd, body=%wide.region_1.5_spmd.sunk | while | flops 102795800 | bytes 8593565 | solution.py:122
  44.0 4.1 all-to-all-start.2
  54.5 76.6 %while.46 = (s32[]{:T(128)}, f32[8,128,512]{2,1,0:T(8,128)}, bf16[4,128,256]{2,1,0:T(8,128)(2,1)}, s32[4,4]{1,0:T(4,128)}, bf16[4,128,4,64]{1,3,2,0:T(8,128)(2,1...) while((s32[]{:T(128)}, f32[8,128,512]{2,1,0:T(8,128)}, ...), condition=%wide.region_15.17_spmd, body=%wide.region_10.16_spmd.sunk | while | flops 174853664 | bytes 29198212 | solution.py:144
  63.1 4.2 fusion.256
  82.3 4.2 fusion.256
  101.4 4.2 fusion.256
  120.6 4.2 fusion.256
  134.5 4.4 %all_to_all.59 = bf16[2,512,256]{2,1,0:T(8,128)(2,1)S(1)} all-to-all(bf16[2,512,256]{2,1,0:T(8,128)(2,1)S(1)} %bitcast.361), channel_id=1, replica_groups=mesh['pts'=2,'geo_0'=8,'geo_1'=4,'geo_2'=4] {'pts'}, dimensions={0} | all-to-all | bytes 1048576 | tf_op jit(solution)/shard_map/all_to_all | solution.py:40
  145.1 4.4 all-to-all-start.4
  154.0 79.5 %while.47 = (s32[]{:T(128)}, f32[8,128,512]{2,1,0:T(8,128)}, bf16[4,128,256]{2,1,0:T(8,128)(2,1)}, s32[4,4]{1,0:T(4,128)S(1)}, bf16[4,128,4,64]{1,3,2,0:T(8,128)...) while((s32[]{:T(128)}, f32[8,128,512]{2,1,0:T(8,128)}, ...), condition=%wide.region_25.27_spmd, body=%wide.region_20.26_spmd.sunk | while | flops 174853664 | bytes 27085072 | solution.py:144
  159.3 4.1 fusion.266
  164.2 4.2 fusion.265
  179.2 4.1 fusion.266
  184.0 4.2 fusion.265
  203.9 4.2 fusion.265
  223.8 4.2 fusion.265
  237.2 4.7 %all-to-all-start.5 = ((bf16[2,512,256]{2,1,0:T(8,128)(2,1)}), bf16[2,512,256]{2,1,0:T(8,128)(2,1)}, u32[]{:S(2)}, u32[]{:S(2)}) async-start(bf16[2,512,256]{2,1,0:T(8,128)(2,1)} %bitcast.360), calls=%async_computation.5 | async-start | bytes 1048576 | tf_op jit(solution)/shard_map/all_to_all | solution.py:40
  258.6 25.5 %while.45 = (s32[]{:T(128)}, bf16[4,128,256]{2,1,0:T(8,128)(2,1)}, s32[4,4]{1,0:T(4,128)}, bf16[8,128,512]{2,1,0:T(8,128)(2,1)S(1)}, bf16[4,128,4,64]{1,3,2,0:T(8,128)(2,1)}, /*index=5*/s32[]{:T(128)}) while((s32[]{:T(128)}, bf16[4,128,256]{2,1,0:T(8,128)(2,1)}, s32[4,4]{1,0:T(4,128)}, bf16[8,128,512]{2,1,0:T(8,128)(2,1)S(1)}, ...), condition=%wide.region_9.11_spmd, body=%wide.region_6.10_spmd.sunk | while | flops 102795800 | bytes 8595089 | solution.py:122
  299.7 30.0 %all_to_all.60 = f32[4,64,2050]{2,1,0:T(8,128)S(1)} all-to-all(f32[4,64,2050]{2,1,0:T(8,128)S(1)} %copy.124), channel_id=1, replica_groups=mesh['pts'=2,'geo_0'=8,'geo_1'=4,'geo_2'=4] {'geo_2'}, dimensions={0} | all-to-all | bytes 4198400 | tf_op jit(solution)/shard_map/all_to_all | solution.py:46
  330.3 30.4 %all_to_all.61 = f32[64,1,2050]{2,1,0:T(1,128)S(1)} all-to-all(f32[64,1,2050]{2,1,0:T(1,128)S(1)} %all_to_all.43), channel_id=1, replica_groups=mesh['pts'=2,'geo_0'=8,'geo_1'=4,'geo_2'=4] {'pts','geo_0','geo_1'}, dimensions={0} | all-to-all | bytes 1049600 | tf_op jit(solution)/shard_map/all_to_all | solution.py:54
  361.3 23.9 %all_to_all.58 = f32[64,1,2050]{2,1,0:T(1,128)S(1)} all-to-all(f32[64,1,2050]{2,1,0:T(1,128)S(1)} %broadcast_in_dim.86), channel_id=1, replica_groups=mesh['pts'=2,'geo_0'=8,'geo_1'=4,'geo_2'=4] {'pts','geo_0','geo_1'}, dimensions={0} | all-to-all | bytes 1049600 | tf_op jit(solution)/shard_map/all_to_all | solution.py:19
  386.7 4.6 %all-to-all-start.9 = ((f32[4,64,2050]{2,1,0:T(8,128)}), f32[4,64,2050]{2,1,0:T(8,128)}, u32[]{:S(2)}, u32[]{:S(2)}) async-start(f32[4,64,2050]{2,1,0:T(8,128)} %broadcast_in_dim.87), calls=%async_computation.9 | async-start | bytes 4456448 | tf_op jit(solution)/shard_map/all_to_all | solution.py:19
  393.3 26.3 %all-to-all-done.9 = f32[4,64,2050]{2,1,0:T(8,128)} async-done(((f32[4,64,2050]{2,1,0:T(8,128)}), f32[4,64,2050]{2,1,0:T(8,128)}, u32[]{:S(2)}, u32[]{:S(2)}) %all-to-all-start.9) | async-done | bytes 2099232 | tf_op jit(solution)/shard_map/all_to_all | solution.py:19
  (460 shorter events, 252.3 us)
Async XLA Ops:
  0.6 33.1 %copy-start = (bf16[256,256]{1,0:T(8,128)(2,1)S(1)}, bf16[256,256]{1,0:T(8,128)(2,1)}, u32[]{:S(2)}) copy-start(bf16[256,256]{1,0:T(8,128)(2,1)} %param.28) | copy-start | bytes 393220
  0.6 11.0 %copy-start.25 = (bf16[256,768]{1,0:T(8,128)(2,1)S(1)}, bf16[256,768]{1,0:T(8,128)(2,1)}, u32[]{:S(2)}) copy-start(bf16[256,768]{1,0:T(8,128)(2,1)} %param.27) | copy-start | bytes 1179652
  5.0 8.1 %all-to-all-start = ((bf16[2,512,256]{2,1,0:T(8,128)(2,1)}), bf16[2,512,256]{2,1,0:T(8,128)(2,1)S(1)}, u32[]{:S(2)}, u32[]{:S(2)}) async-start(bf16[2,512,256]{2,1,0:T(8,128)(2,1)} %broadcast_in_dim.79), calls=%async_computation | async-start | bytes 1048576 | tf_op jit(solution)/shard_map/all_to_all | solution.py:19
  15.0 18.7 %copy-start.4 = (bf16[1,512,256]{2,1,0:T(8,128)(2,1)S(1)}, bf16[1,512,256]{2,1,0:T(8,128)(2,1)}, u32[]{:S(2)}) copy-start(bf16[1,512,256]{2,1,0:T(8,128)(2,1)} %param.21) | copy-start | bytes 786436
  33.7 8.3 %copy-start.19 = (bf16[4,128,256]{2,1,0:T(8,128)(2,1)}, bf16[4,128,256]{2,1,0:T(8,128)(2,1)S(1)}, u32[]{:S(2)}) copy-start(bf16[4,128,256]{2,1,0:T(8,128)(2,1)S(1)} %get-tuple-element.139) | copy-start | bytes 786436
  33.7 8.3 %copy-start.29 = (bf16[4,128,4,64]{1,3,2,0:T(8,128)(2,1)}, bf16[4,128,4,64]{1,3,2,0:T(8,128)(2,1)S(1)}, u32[]{:S(2)}) copy-start(bf16[4,128,4,64]{1,3,2,0:T(8,128)(2,1)S(1)} %get-tuple-element.603) | copy-start | bytes 786436
  34.0 8.9 %copy-start.46 = (bf16[256]{0:T(256)(128)(2,1)S(1)}, bf16[256]{0:T(256)(128)(2,1)}, u32[]{:S(2)}) copy-start(bf16[256]{0:T(256)(128)(2,1)} %param.29) | copy-start | bytes 1540
  34.8 5.2 %all-to-all-start.1 = ((bf16[2,512,256]{2,1,0:T(8,128)(2,1)}), bf16[2,512,256]{2,1,0:T(8,128)(2,1)S(1)}, u32[]{:S(2)}, u32[]{:S(2)}) async-start(bf16[2,512,256]{2,1,0:T(8,128)(2,1)} %broadcast_in_dim.80), calls=%async_computation.1 | async-start | bytes 1048576 | tf_op jit(solution)/shard_map/all_to_all | solution.py:19
  40.1 8.1 %copy-start.24 = (bf16[256,768]{1,0:T(8,128)(2,1)S(1)}, bf16[256,768]{1,0:T(8,128)(2,1)}, u32[]{:S(2)}) copy-start(bf16[256,768]{1,0:T(8,128)(2,1)} %param.30) | copy-start | bytes 1179652
  43.1 6.8 %copy-start.10 = (bf16[512,256]{1,0:T(8,128)(2,1)}, bf16[512,256]{1,0:T(8,128)(2,1)S(1)}, u32[]{:S(2)}) copy-start(bf16[512,256]{1,0:T(8,128)(2,1)S(1)} %fusion.127) | copy-start | bytes 786436
  44.0 5.5 %all-to-all-start.2 = ((bf16[2,512,256]{2,1,0:T(8,128)(2,1)}), bf16[2,512,256]{2,1,0:T(8,128)(2,1)S(1)}, u32[]{:S(2)}, u32[]{:S(2)}) async-start(bf16[2,512,256]{2,1,0:T(8,128)(2,1)} %broadcast_in_dim.82), calls=%async_computation.2 | async-start | bytes 1048576 | tf_op jit(solution)/shard_map/all_to_all | solution.py:19
  54.5 8.6 %copy-start.26 = (bf16[4,128,4,64]{1,3,2,0:T(8,128)(2,1)}, bf16[4,128,4,64]{1,3,2,0:T(8,128)(2,1)S(1)}, u32[]{:S(2)}) copy-start(bf16[4,128,4,64]{1,3,2,0:T(8,128)(2,1)S(1)} %get-tuple-element.567) | copy-start | bytes 786436 | tf_op jit(solution)/shard_map/while
  73.6 8.7 %copy-start.26 = (bf16[4,128,4,64]{1,3,2,0:T(8,128)(2,1)}, bf16[4,128,4,64]{1,3,2,0:T(8,128)(2,1)S(1)}, u32[]{:S(2)}) copy-start(bf16[4,128,4,64]{1,3,2,0:T(8,128)(2,1)S(1)} %get-tuple-element.567) | copy-start | bytes 786436 | tf_op jit(solution)/shard_map/while
  92.8 8.7 %copy-start.26 = (bf16[4,128,4,64]{1,3,2,0:T(8,128)(2,1)}, bf16[4,128,4,64]{1,3,2,0:T(8,128)(2,1)S(1)}, u32[]{:S(2)}) copy-start(bf16[4,128,4,64]{1,3,2,0:T(8,128)(2,1)S(1)} %get-tuple-element.567) | copy-start | bytes 786436 | tf_op jit(solution)/shard_map/while
  112.0 8.7 %copy-start.26 = (bf16[4,128,4,64]{1,3,2,0:T(8,128)(2,1)}, bf16[4,128,4,64]{1,3,2,0:T(8,128)(2,1)S(1)}, u32[]{:S(2)}) copy-start(bf16[4,128,4,64]{1,3,2,0:T(8,128)(2,1)S(1)} %get-tuple-element.567) | copy-start | bytes 786436 | tf_op jit(solution)/shard_map/while
  134.5 5.7 %copy-start.39 = (f32[256]{0:T(256)S(1)}, f32[256]{0:T(256)}, u32[]{:S(2)}) copy-start(f32[256]{0:T(256)} %copy-done.38) | copy-start | bytes 3076
  134.5 6.6 %copy-start.17 = (bf16[1,512,256]{2,1,0:T(8,128)(2,1)S(1)}, bf16[1,512,256]{2,1,0:T(8,128)(2,1)}, u32[]{:S(2)}) copy-start(bf16[1,512,256]{2,1,0:T(8,128)(2,1)} %param.22) | copy-start | bytes 786436
  145.1 5.7 %all-to-all-start.4 = ((bf16[2,512,256]{2,1,0:T(8,128)(2,1)}), bf16[2,512,256]{2,1,0:T(8,128)(2,1)S(1)}, u32[]{:S(2)}, u32[]{:S(2)}) async-start(bf16[2,512,256]{2,1,0:T(8,128)(2,1)} %bitcast.56), calls=%async_computation.4 | async-start | bytes 1048576 | tf_op jit(solution)/shard_map/all_to_all | solution.py:40
  233.6 8.4 %copy-start.2 = (f32[8,128,512]{2,1,0:T(8,128)S(1)}, f32[8,128,512]{2,1,0:T(8,128)}, u32[]{:S(2)}) copy-start(f32[8,128,512]{2,1,0:T(8,128)} %get-tuple-element.142) | copy-start | bytes 6291460
  237.2 16.5 %all-to-all-start.5 = ((bf16[2,512,256]{2,1,0:T(8,128)(2,1)}), bf16[2,512,256]{2,1,0:T(8,128)(2,1)}, u32[]{:S(2)}, u32[]{:S(2)}) async-start(bf16[2,512,256]{2,1,0:T(8,128)(2,1)} %bitcast.360), calls=%async_computation.5 | async-start | bytes 1048576 | tf_op jit(solution)/shard_map/all_to_all | solution.py:40
  284.1 6.9 %copy-start.45 = (f32[256]{0:T(256)S(1)}, f32[256]{0:T(256)}, u32[]{:S(2)}) copy-start(f32[256]{0:T(256)} %get-tuple-element.265) | copy-start | bytes 3076
  284.1 8.2 %copy-start.15 = (f32[196608]{0:T(1024)S(1)}, f32[196608]{0:T(1024)}, u32[]{:S(2)}) copy-start(f32[196608]{0:T(1024)} %reshape.305) | copy-start | bytes 2359300
  386.7 5.6 %copy-start.14 = (bf16[512,256]{1,0:T(8,128)(2,1)S(1)}, bf16[512,256]{1,0:T(8,128)(2,1)}, u32[]{:S(2)}) copy-start(bf16[512,256]{1,0:T(8,128)(2,1)} %copy-done.12) | copy-start | bytes 786436
  386.7 32.8 %all-to-all-start.9 = ((f32[4,64,2050]{2,1,0:T(8,128)}), f32[4,64,2050]{2,1,0:T(8,128)}, u32[]{:S(2)}, u32[]{:S(2)}) async-start(f32[4,64,2050]{2,1,0:T(8,128)} %broadcast_in_dim.87), calls=%async_computation.9 | async-start | bytes 4456448 | tf_op jit(solution)/shard_map/all_to_all | solution.py:19
  (55 other events, 203.9 us)
where the time goes:
time: 444 us; the launch traced here: 436 us
  matrix products  143 us (32%)
  local copies, waits for them, and re-layouts  92 us (21%)
  blocking collectives  88.6 us (20%)
  other arithmetic  50.7 us (11%)
  waiting for transfers between devices  30.6 us (7%)
  starting transfers between devices  28.3 us (6%)
    dot_general x8, matrix products, ball_backward(): jnp.einsum('hqk,qhd->khd', scores_grad, query_ball, preferred_element_typ...  33.5 us
    dot_general x8, matrix products, ball_backward(): jnp.einsum('hqk,khd->qhd', scores_grad, keys, preferred_element_type=jnp....  32.6 us
    all_to_all x1, blocking collectives, sum_in_two_steps(): lax.all_to_all(nearer, far, split_axis=0, concat_axis=0, tiled=True)  30.4 us
    all_to_all x1, blocking collectives, sent_and_summed(): lax.all_to_all(cut_along(array, dim, length), axis, 0, 0, tiled=True)  30 us
    all_to_all x4, waiting for transfers between devices, from_everyone(): return lax.all_to_all(copies, axis, split_axis=0, concat_axis=0, tiled=True)  29.3 us
    scatter-add x8, other arithmetic, one_ball(): buffer = buffer.at[chosen_ids].add(stacked)  25.2 us
    all_to_all x1, blocking collectives, from_everyone(): return lax.all_to_all(copies, axis, split_axis=0, concat_axis=0, tiled=True)  23.9 us
    sub x16, matrix products, ball_softmax(): exponent = jnp.exp(scores - topmost)  23.2 us
  transfers between devices with their start and end apart: 6, of which 5 were waited for; matrix products, arithmetic and copies ran while one was open for 3% of the time, Pallas kernels for 0%

commit v1 on v0

v1 whole, which is shorter than its diff:
```python
import functools

import jax
import jax.numpy as jnp
from jax import lax
from jax.experimental import pallas as pl
from jax.experimental.pallas import tpu as pltpu
from jax.sharding import PartitionSpec as P

HEADS = 4
BALL = 128
LISTED = 4
BALLS = 8
ROWS = BALL * BALLS
HALF = ROWS // 2
D = 256
OWN = 128
EPSILON = 1e-06
XY = 16
WIDE = 1152
CHUNK = 256 // XY
MESH = pl.DeviceIdType.MESH
F32 = jnp.float32
BF16 = jnp.bfloat16


def dot(a, b):
    return jnp.dot(a, b, preferred_element_type=F32)


def dot_nt(a, b):
    return lax.dot_general(a, b, (((1,), (1,)), ((), ())), preferred_element_type=F32)


def rows_of(b, size=BALL):
    return pl.ds(pl.multiple_of(b * size, size), size)


def layers_kernel(
    points,
    result_grad,
    lists_one,
    lists_two,
    rotation,
    gain_one,
    qkv_one,
    out_one,
    gain_two,
    qkv_two,
    out_two,
    result,
    points_grad,
    packed,
    x_all,
    g_all,
    lists_v,
    lists_s,
    rot_v,
    w_own,
    normed_t,
    q_st,
    kv_all,
    k_t,
    v_t,
    att,
    mix_t,
    mixed,
    dqkv,
    parts,
    ngrad,
    perm,
    perm_t,
    in_send,
    in_recv,
    own_sem,
    smem_sem,
    mix_send,
    mix_recv,
    ng_send,
    ng_recv,
):
    c = lax.axis_index("pts")
    other = 1 - c
    gains = (gain_one, gain_two)
    qkvs = (qkv_one, qkv_two)
    outs = (out_one, out_two)

    def remote(src, dst, send, recv):
        return pltpu.make_async_remote_copy(
            src_ref=src,
            dst_ref=dst,
            send_sem=send,
            recv_sem=recv,
            device_id={"pts": other},
            device_id_type=MESH,
        )

    barrier = pltpu.get_barrier_semaphore()
    pl.semaphore_signal(barrier, inc=1, device_id={"pts": other}, device_id_type=MESH)
    pl.semaphore_wait(barrier, 1)

    inputs = (
        (points.at[0], x_all.at[0, rows_of(c, HALF)]),
        (lists_one.at[0], lists_v.at[0, c]),
        (lists_two.at[0], lists_v.at[1, c]),
        (rotation, rot_v.at[c]),
        (result_grad.at[0], g_all.at[1, rows_of(c, HALF)]),
    )
    sent = [
        remote(src, dst, in_send.at[n], in_recv.at[n]) for n, (src, dst) in enumerate(inputs)
    ]
    kept = [
        pltpu.make_async_copy(src, dst, own_sem.at[n]) for n, (src, dst) in enumerate(inputs)
    ]
    for copy in sent:
        copy.start()
    for copy in kept:
        copy.start()

    col = pl.ds(pl.multiple_of(c * OWN, OWN), OWN)
    for i in range(2):
        for n in range(3):
            part = pl.ds(pl.multiple_of(n * D + c * OWN, OWN), OWN)
            w_own[i, :, n * OWN : (n + 1) * OWN] = qkvs[i][:, part]
    parts[LISTED * BALLS] = jnp.zeros((BALL, D), F32)

    lane = lax.broadcasted_iota(jnp.int32, (BALL, OWN), 1)
    first = lane < OWN // 2

    def stacked(value):
        zero = jnp.zeros_like(value)
        return jnp.concatenate(
            [jnp.where(first, value, zero), jnp.where(first, zero, value)], axis=0
        )

    def unstacked_t(value):
        return jnp.concatenate([value[: OWN // 2, :BALL], value[OWN // 2 :, BALL:]], axis=0)

    def project(i, b):
        x = x_all[i, rows_of(b)].astype(F32)
        gain = gains[i][...].astype(F32)
        factor = lax.rsqrt(jnp.mean(x * x, axis=-1, keepdims=True) + EPSILON)
        normed = x * factor * gain
        normed_t[i, :, rows_of(b)] = normed.T.astype(BF16)
        qkv = dot(normed.astype(BF16), w_own[i])
        q = qkv[:, :OWN].astype(BF16).astype(F32) * 0.125
        q_st[i, b] = stacked(q).astype(BF16)
        kv_all[i, b] = qkv[:, OWN:].astype(BF16)
        k_t[i, b] = qkv[:, OWN : 2 * OWN].T.astype(BF16)
        v_t[i, b] = qkv[:, 2 * OWN :].T.astype(BF16)

    def listed(i, b):
        return [lists_s[i, b // 4, b % 4, n] for n in range(LISTED)]

    def attend(i, b):
        ids = listed(i, b)
        keys = jnp.concatenate([kv_all[i, t, :, :OWN] for t in ids], axis=0)
        scores = dot_nt(keys, q_st[i, b])
        top = jnp.max(scores, axis=0, keepdims=True)
        exponent = jnp.exp(scores - top)
        attention = exponent * (1.0 / jnp.sum(exponent, axis=0, keepdims=True))
        att[i, b] = attention
        values_t = jnp.concatenate([v_t[i, t] for t in ids], axis=1)
        own_t = unstacked_t(dot(values_t, attention.astype(BF16)))
        mix_t[i, :, rows_of(b)] = own_t.astype(BF16)
        mixed[i, c, rows_of(b)] = own_t.T.astype(BF16)

    def mix_copy(i, b, slot):
        ref = mixed.at[i, c, rows_of(b)]
        return remote(ref, ref, mix_send.at[i, slot], mix_recv.at[i, slot])

    def project_out(i, b):
        both = jnp.concatenate([mixed[i, 0, rows_of(b)], mixed[i, 1, rows_of(b)]], axis=1)
        x = x_all[i, rows_of(b)].astype(F32)
        return (x + dot(both, outs[i][...])).astype(BF16)

    kept[0].wait()
    lax.fori_loop(0, 4, lambda j, _: project(0, c * 4 + j), None)
    for n in (1, 2, 3):
        kept[n].wait()
        sent[n].wait()
    to_smem = pltpu.make_async_copy(lists_v, lists_s, smem_sem)
    to_smem.start()
    sent[0].wait()
    lax.fori_loop(0, 4, lambda j, _: project(0, other * 4 + j), None)
    to_smem.wait()

    def attend_send(j, _):
        attend(0, j)
        mix_copy(0, j, j).start()

    lax.fori_loop(0, BALLS, attend_send, None)

    rot_row = jnp.concatenate([rot_v[0], rot_v[1]], axis=1)

    def build_t(b, _):
        ids = lax.broadcasted_iota(jnp.int32, (BALL, ROWS), 0) + b * BALL
        perm_t[rows_of(b)] = jnp.where(ids == rot_row, 1.0, 0.0).astype(BF16)

    lax.fori_loop(0, BALLS, build_t, None)
    for b in range(BALLS):
        here = rot_row[:, b * BALL : (b + 1) * BALL].astype(F32)
        column = jnp.broadcast_to(here, (BALL, BALL)).T
        for n in range(BALLS):
            ids = (lane + n * BALL).astype(F32)
            perm[b * BALL : (b + 1) * BALL, n * BALL : (n + 1) * BALL] = jnp.where(
                ids == column, 1.0, 0.0
            ).astype(BF16)

    def hidden_rows(b, _):
        mix_copy(0, b, b).wait()
        x_all[2, rows_of(b)] = project_out(0, b)

    lax.fori_loop(0, BALLS, hidden_rows, None)

    def rotate(b, _):
        x_all[1, rows_of(b)] = dot(perm[rows_of(b)], x_all[2]).astype(BF16)
        project(1, b)

    lax.fori_loop(0, BALLS, rotate, None)

    def attend_two(j, _):
        attend(1, other * 4 + j)
        mix_copy(1, other * 4 + j, j).start()

    lax.fori_loop(0, 4, attend_two, None)
    lax.fori_loop(0, 4, lambda j, _: attend(1, c * 4 + j), None)

    def result_rows(j, _):
        mix_copy(1, other * 4 + j, j).wait()
        result[0, rows_of(j)] = project_out(1, c * 4 + j)

    lax.fori_loop(0, 4, result_rows, None)
    kept[4].wait()
    sent[4].wait()

    def attend_back(i, b):
        ids = listed(i, b)
        mixed_grad = stacked(dot_nt(g_all[i, rows_of(b)], outs[i][col, :])).astype(BF16)
        values = jnp.concatenate([kv_all[i, t, :, OWN:] for t in ids], axis=0)
        weights_grad = dot_nt(values, mixed_grad)
        attention = att[i, b]
        inner = jnp.sum(attention * weights_grad, axis=0, keepdims=True)
        scores_grad = (attention * (weights_grad - inner)).astype(BF16)
        values_grad = dot(attention.astype(BF16), mixed_grad)
        keys_grad = dot(scores_grad, q_st[i, b])
        for n in range(LISTED):
            parts[b * LISTED + n, :, :OWN] = keys_grad[n * BALL : (n + 1) * BALL]
            parts[b * LISTED + n, :, OWN:] = values_grad[n * BALL : (n + 1) * BALL]
        keys_t = jnp.concatenate([k_t[i, t] for t in ids], axis=1)
        query_grad_t = unstacked_t(dot(keys_t, scores_grad)) * 0.125
        dqkv[rows_of(b), :OWN] = query_grad_t.T.astype(BF16)

    def gather_parts(i, t):
        total = jnp.zeros((BALL, D), F32)
        for b in range(BALLS):
            at = jnp.int32(LISTED * BALLS)
            for n in range(LISTED):
                at = jnp.where(lists_s[i, b // 4, b % 4, n] == t, b * LISTED + n, at)
            total = total + parts[at]
        dqkv[rows_of(t), OWN:] = total.astype(BF16)

    def ng_copy(i, b, slot):
        ref = ngrad.at[i, c, rows_of(b)]
        return remote(ref, ref, ng_send.at[i, slot], ng_recv.at[i, slot])

    def partial_rows(i, b):
        ngrad[i, c, rows_of(b)] = dot_nt(dqkv[rows_of(b)], w_own[i]).astype(BF16)

    def weight_grads(i):
        at = i * 512
        weight = dot(normed_t[i], dqkv[...]).astype(BF16)
        packed[:, at : at + 3 * OWN] = weight
        out_grad = dot(mix_t[i], g_all[i]).astype(BF16)
        packed[:OWN, at + 3 * OWN : at + 4 * OWN] = out_grad[:, :OWN]
        packed[OWN:, at + 3 * OWN : at + 4 * OWN] = out_grad[:, OWN:]

    def row_grads(i, b):
        x = x_all[i, rows_of(b)].astype(F32)
        gain = gains[i][...].astype(F32)
        factor = lax.rsqrt(jnp.mean(x * x, axis=-1, keepdims=True) + EPSILON)
        grad = ngrad[i, 0, rows_of(b)].astype(F32) + ngrad[i, 1, rows_of(b)].astype(F32)
        grad = grad.astype(BF16).astype(F32)
        scaled = grad * gain
        inner = jnp.mean(scaled * x, axis=-1, keepdims=True)
        inputs_grad = factor * scaled - x * (factor * factor * factor) * inner
        rows = (g_all[i, rows_of(b)].astype(F32) + inputs_grad).astype(BF16)
        return rows, jnp.sum(grad * (x * factor), axis=0, keepdims=True)

    lax.fori_loop(0, BALLS, lambda b, _: attend_back(1, b), None)
    lax.fori_loop(0, BALLS, lambda t, _: gather_parts(1, t), None)

    def partial_two(b, _):
        partial_rows(1, b)
        ng_copy(1, b, b).start()

    lax.fori_loop(0, BALLS, partial_two, None)
    weight_grads(1)

    def rows_two(b, total):
        ng_copy(1, b, b).wait()
        rows, gain_part = row_grads(1, b)
        x_all[2, rows_of(b)] = rows
        mine = ((b // 4) == c).astype(F32)
        return total + gain_part * mine

    gain_two_part = lax.fori_loop(0, BALLS, rows_two, jnp.zeros((1, D), F32))

    def unrotate(b, _):
        g_all[0, rows_of(b)] = dot(perm_t[rows_of(b)], x_all[2]).astype(BF16)

    lax.fori_loop(0, BALLS, unrotate, None)
    lax.fori_loop(0, BALLS, lambda b, _: attend_back(0, b), None)
    lax.fori_loop(0, BALLS, lambda t, _: gather_parts(0, t), None)

    def partial_one(j, _):
        partial_rows(0, other * 4 + j)
        ng_copy(0, other * 4 + j, j).start()

    lax.fori_loop(0, 4, partial_one, None)
    lax.fori_loop(0, 4, lambda j, _: partial_rows(0, c * 4 + j), None)
    weight_grads(0)

    def rows_one(j, total):
        ng_copy(0, other * 4 + j, j).wait()
        rows, gain_part = row_grads(0, c * 4 + j)
        points_grad[0, rows_of(j)] = rows
        return total + gain_part

    gain_one_part = lax.fori_loop(0, 4, rows_one, jnp.zeros((1, D), F32))
    one = jnp.broadcast_to(gain_one_part, (OWN, D)).T
    two = jnp.broadcast_to(gain_two_part, (OWN, D)).T
    wide = lax.broadcasted_iota(jnp.int32, (D, OWN), 1)
    packed[:, 1024:] = jnp.where(wide < OWN // 2, one, two).astype(BF16)


def sum_kernel(
    planes,
    packed,
    gain_one,
    qkv_one,
    out_one,
    gain_two,
    qkv_two,
    out_two,
    arrived,
    along_z,
    full,
    send_xy,
    recv_xy,
    send_z,
    recv_z,
    send_all,
    recv_all,
    send_core,
    recv_core,
):
    c = lax.axis_index("pts")
    geo = lax.axis_index("geo")
    z = geo // XY
    xy = geo % XY

    def near(k):
        return {"geo": z * XY + (xy + k) % XY}

    def deep(k):
        return {"geo": ((z + k) % planes) * XY + xy}

    def remote(src, dst, send, recv, device):
        return pltpu.make_async_remote_copy(
            src_ref=src,
            dst_ref=dst,
            send_sem=send,
            recv_sem=recv,
            device_id=device,
            device_id_type=MESH,
        )

    barrier = pltpu.get_barrier_semaphore()
    for k in range(1, XY):
        pl.semaphore_signal(barrier, inc=1, device_id=near(k), device_id_type=MESH)
    for k in range(1, planes):
        pl.semaphore_signal(barrier, inc=1, device_id=deep(k), device_id_type=MESH)
    pl.semaphore_signal(barrier, inc=1, device_id={"pts": 1 - c}, device_id_type=MESH)
    pl.semaphore_wait(barrier, XY + planes - 1)

    first = []
    for k in range(1, XY):
        peer = (xy + k) % XY
        first.append(
            remote(
                packed.at[rows_of(peer, CHUNK)],
                arrived.at[k - 1],
                send_xy.at[k - 1],
                recv_xy.at[k - 1],
                near(k),
            )
        )
        first[-1].start()
    total = packed[rows_of(xy, CHUNK)].astype(F32)
    for k in range(1, XY):
        first[k - 1].wait()
        total = total + arrived[k - 1].astype(F32)
    along_z[z] = total.astype(BF16)

    second = []
    for k in range(1, planes):
        second.append(
            remote(
                along_z.at[z], along_z.at[z], send_z.at[k - 1], recv_z.at[k - 1], deep(k)
            )
        )
        second[-1].start()
    for copy in second:
        copy.wait()
    total = along_z[0].astype(F32)
    for k in range(1, planes):
        total = total + along_z[k].astype(F32)
    full[c, rows_of(xy, CHUNK)] = total.astype(BF16)

    mine = full.at[c, rows_of(xy, CHUNK)]
    third = []
    for k in range(1, XY):
        third.append(remote(mine, mine, send_all.at[k - 1], recv_all.at[k - 1], near(k)))
        third[-1].start()
    across = []
    for k in range(XY):
        if k:
            third[k - 1].wait_recv()
        piece = full.at[c, rows_of((xy - k + XY) % XY, CHUNK)]
        across.append(
            remote(piece, piece, send_core.at[k], recv_core.at[k], {"pts": 1 - c})
        )
        across[-1].start()
    for copy in third:
        copy.wait_send()
    for copy in across:
        copy.wait()

    for at, qkv, out in ((0, qkv_one, out_one), (512, qkv_two, out_two)):
        for core in range(2):
            for n in range(3):
                qkv[:, n * D + core * OWN : n * D + (core + 1) * OWN] = full[
                    core, :, at + n * OWN : at + (n + 1) * OWN
                ].astype(F32)
            here = slice(core * OWN, (core + 1) * OWN)
            out[here, :OWN] = full[core, :OWN, at + 3 * OWN : at + 4 * OWN].astype(F32)
            out[here, OWN:] = full[core, OWN:, at + 3 * OWN : at + 4 * OWN].astype(F32)
    gains = (full[0, :, 1024:].astype(F32) + full[1, :, 1024:].astype(F32)).T
    gain_one[...] = gains[:1]
    gain_two[...] = gains[OWN // 2 : OWN // 2 + 1]


def vmem():
    return pl.BlockSpec(memory_space=pltpu.VMEM)


def layers_call(*args):
    return pl.pallas_call(
        layers_kernel,
        name="layers",
        out_shape=(
            jax.ShapeDtypeStruct((1, HALF, D), BF16),
            jax.ShapeDtypeStruct((1, HALF, D), BF16),
            jax.ShapeDtypeStruct((D, WIDE), BF16),
        ),
        in_specs=[vmem()] * 11,
        out_specs=(vmem(),) * 3,
        scratch_shapes=[
            pltpu.VMEM((3, ROWS, D), BF16),
            pltpu.VMEM((2, ROWS, D), BF16),
            pltpu.VMEM((2, 2, 4, LISTED), jnp.int32),
            pltpu.SMEM((2, 2, 4, LISTED), jnp.int32),
            pltpu.VMEM((2, 1, HALF), jnp.int32),
            pltpu.VMEM((2, D, 3 * OWN), BF16),
            pltpu.VMEM((2, D, ROWS), BF16),
            pltpu.VMEM((2, BALLS, 2 * BALL, OWN), BF16),
            pltpu.VMEM((2, BALLS, BALL, 2 * OWN), BF16),
            pltpu.VMEM((2, BALLS, OWN, BALL), BF16),
            pltpu.VMEM((2, BALLS, OWN, BALL), BF16),
            pltpu.VMEM((2, BALLS, LISTED * BALL, 2 * BALL), F32),
            pltpu.VMEM((2, OWN, ROWS), BF16),
            pltpu.VMEM((2, 2, ROWS, OWN), BF16),
            pltpu.VMEM((ROWS, 3 * OWN), BF16),
            pltpu.VMEM((LISTED * BALLS + 1, BALL, D), F32),
            pltpu.VMEM((2, 2, ROWS, D), BF16),
            pltpu.VMEM((ROWS, ROWS), BF16),
            pltpu.VMEM((ROWS, ROWS), BF16),
            pltpu.SemaphoreType.DMA((5,)),
            pltpu.SemaphoreType.DMA((5,)),
            pltpu.SemaphoreType.DMA((5,)),
            pltpu.SemaphoreType.DMA,
            pltpu.SemaphoreType.DMA((2, BALLS)),
            pltpu.SemaphoreType.DMA((2, BALLS)),
            pltpu.SemaphoreType.DMA((2, BALLS)),
            pltpu.SemaphoreType.DMA((2, BALLS)),
        ],
        compiler_params=pltpu.CompilerParams(
            collective_id=0, has_side_effects=True, vmem_limit_bytes=56 << 20
        ),
    )(*args)


def sums_call(packed, planes):
    shapes = (
        jax.ShapeDtypeStruct((1, D), F32),
        jax.ShapeDtypeStruct((D, 3 * D), F32),
        jax.ShapeDtypeStruct((D, D), F32),
    )
    return pl.pallas_call(
        functools.partial(sum_kernel, planes),
        name="sums",
        out_shape=shapes + shapes,
        in_specs=[vmem()],
        out_specs=(vmem(),) * 6,
        scratch_shapes=[
            pltpu.VMEM((XY - 1, CHUNK, WIDE), BF16),
            pltpu.VMEM((planes, CHUNK, WIDE), BF16),
            pltpu.VMEM((2, D, WIDE), BF16),
            pltpu.SemaphoreType.DMA((XY - 1,)),
            pltpu.SemaphoreType.DMA((XY - 1,)),
            pltpu.SemaphoreType.DMA((max(planes - 1, 1),)),
            pltpu.SemaphoreType.DMA((max(planes - 1, 1),)),
            pltpu.SemaphoreType.DMA((XY - 1,)),
            pltpu.SemaphoreType.DMA((XY - 1,)),
            pltpu.SemaphoreType.DMA((XY,)),
            pltpu.SemaphoreType.DMA((XY,)),
        ],
        compiler_params=pltpu.CompilerParams(
            collective_id=1, has_side_effects=True, vmem_limit_bytes=32 << 20
        ),
    )(packed)


def local(
    points,
    result_grad,
    lists_one,
    lists_two,
    rotation,
    gain_one,
    qkv_one,
    out_one,
    gain_two,
    qkv_two,
    out_two,
):
    result, points_grad, packed = layers_call(
        points,
        result_grad,
        lists_one,
        lists_two,
        rotation,
        gain_one.reshape(1, D),
        qkv_one,
        out_one,
        gain_two.reshape(1, D),
        qkv_two,
        out_two,
    )
    grads = sums_call(packed, lax.axis_size("geo") // XY)
    return (
        result,
        points_grad,
        grads[0].reshape(D),
        grads[1],
        grads[2],
        grads[3].reshape(D),
        grads[4],
        grads[5],
    )


def solution(mesh):
    rows = P("geo", "pts", None)
    placed = (rows, rows, rows, rows, P("geo", "pts"), P(), P(), P(), P(), P(), P())
    return jax.shard_map(
        local,
        mesh=mesh,
        in_specs=placed,
        out_specs=(rows, rows, P(), P(), P(), P(), P(), P()),
        check_vma=False,
    )
```

time: 444 us -> 96.5 us (0.22); the launches traced: 436 us -> 96.3 us
  matrix products: 143 us -> 0 us
  blocking collectives: 88.6 us -> 0 us
  Pallas kernels: 0 us -> 86.7 us
  local copies, waits for them, and re-layouts: 92 us -> 8.88 us
  other arithmetic: 50.7 us -> 0 us
  waiting for transfers between devices: 30.6 us -> 0 us
  starting transfers between devices: 28.3 us -> 0 us
    dot_general x66 -> x0, matrix products: 120 us -> none  [the longest x8 33.5 us: ball_backward(): jnp.einsum('hqk,qhd->khd', scores_grad, query_ball, preferred_element_typ...]
    all_to_all x4 -> x0, blocking collectives: 88.6 us -> none  [the longest x1 30.4 us: sum_in_two_steps(): lax.all_to_all(nearer, far, split_axis=0, concat_axis=0, tiled=True)]
    pallas_call x0 -> x2, Pallas kernels: none -> 86.7 us  [the longest x1 50 us: layers_call(): pl.pallas_call(layers_kernel, name='layers', out_shape=(jax.ShapeDtypeStr...]
    all_to_all x6 -> x0, waiting for transfers between devices: 30.6 us -> none  [the longest x4 29.3 us: from_everyone(): return lax.all_to_all(copies, axis, split_axis=0, concat_axis=0, tiled=True)]
    all_to_all x6 -> x0, starting transfers between devices: 28.3 us -> none  [the longest x4 19.3 us: from_everyone(): return lax.all_to_all(copies, axis, split_axis=0, concat_axis=0, tiled=True)]
    scatter-add x8 -> x0, other arithmetic: 25.2 us -> none  [one_ball(): buffer = buffer.at[chosen_ids].add(stacked)]
    sub x16 -> x0, matrix products: 23.2 us -> none  [ball_softmax(): exponent = jnp.exp(scores - topmost)]
    gather x17 -> x0, local copies, waits for them, and re-layouts: 21.4 us -> none  [the longest x16 19.5 us: one_ball(): jnp.take(blocks, chosen_ids, axis=0)]
  transfers between devices with their start and end apart: 6 -> 0, of which waited for: 5 -> 0; matrix products, arithmetic and copies ran while one was open for 3% -> 0% of each run, Pallas kernels for 0% -> 0%
where the time goes in v1:
time: 96.5 us; the launch traced here: 96.3 us
  Pallas kernels  86.7 us (90%)
  local copies, waits for them, and re-layouts  8.88 us (9%)
    pallas_call x1, Pallas kernels, layers_call(): pl.pallas_call(layers_kernel, name='layers', out_shape=(jax.ShapeDtypeStr...  50 us
    pallas_call x1, Pallas kernels, sums_call(): pl.pallas_call(functools.partial(sum_kernel, planes), name='sums', out_sh...  36.8 us
    unnamed x16, local copies, waits for them, and re-layouts  7.09 us

profile of v1, /device:TPU:1, one launch (start us, length us, event | category | flops | bytes accessed | tf_op | source)
XLA Modules:
  0.0 96.3 jit_solution(5593048257779802349)
XLA Ops:
  0.6 0.0 copy-start.3
  0.6 1.2 %reshape.28.gain_one = bf16[1,256]{1,0:T(2,128)(2,1)} reshape(bf16[256]{0:T(256)(128)(2,1)} %param.16) | data formatting | bytes 1024 | tf_op jit(solution)/shard_map/reshape | solution.py:554
  1.9 0.0 copy-done.3
  1.9 0.6 reshape.29.gain_two
  2.4 50.0 %layers.1 = (bf16[1,512,256]{2,1,0:T(8,128)(2,1)}, bf16[1,512,256]{2,1,0:T(8,128)(2,1)}, bf16[256,1152]{1,0:T(8,128)(2,1)}) custom-call(bf16[1,512,256]{2,1,0:T(8,128)(2,1)} %points.1, bf16[1,512,256]{2,1,0:T(8,128)(2,1)} %result_grad.1, s32[1,4,4]{2,1,0:T(4,128)} %lists_one.1, s32[1,4,4]{2,1,0:T(4,128)} %lists_two.1, s32[1,512]{1,0:T(1,128)} %rotation.1, ...), custom_call_target="tpu_custom_call" | custom-call | tf_op jit(solution)/shard_map/layers/pallas_call | solution.py:459
  52.4 0.0 copy-start
  52.4 1.1 %copy-done = bf16[256,1152]{1,0:T(8,128)(2,1)S(1)} copy-done((bf16[256,1152]{1,0:T(8,128)(2,1)S(1)}, bf16[256,1152]{1,0:T(8,128)(2,1)}, u32[]{:S(2)}) %copy-start) | copy-done | bytes 589848
  53.5 0.0 copy-start.2
  53.5 36.8 %sums.1 = (f32[1,256]{1,0:T(1,128)S(1)}, f32[256,768]{1,0:T(8,128)S(1)}, f32[256,256]{1,0:T(8,128)S(1)}, f32[1,256]{1,0:T(1,128)S(1)}, f32[256,768]{1,0:T(8,128)S(1)}, /*index=5*/f32[256,256]{1,0:T(8,128)S(1)}) custom-call(bf16[256,1152]{1,0:T(8,128)(2,1)S(1)} %copy-done), custom_call_target="tpu_custom_call" | custom-call | tf_op jit(solution)/shard_map/sums/pallas_call | solution.py:510
  90.3 0.0 copy-done.2
  90.3 0.0 copy-start.1
  90.3 0.7 copy.27
  91.0 0.3 copy-done.1
  91.3 0.7 copy.28
  92.0 0.6 copy.29
  92.6 0.9 copy.30
  93.5 0.7 copy.31
  94.2 0.6 copy.32
  94.7 0.9 copy.33
  95.6 0.7 copy.34
Async XLA Ops:
  0.6 1.2 %copy-start.3 = (bf16[256]{0:T(256)(128)(2,1)S(1)}, bf16[256]{0:T(256)(128)(2,1)}, u32[]{:S(2)}) copy-start(bf16[256]{0:T(256)(128)(2,1)} %param.19) | copy-start | bytes 1540
  52.4 1.1 %copy-start = (bf16[256,1152]{1,0:T(8,128)(2,1)S(1)}, bf16[256,1152]{1,0:T(8,128)(2,1)}, u32[]{:S(2)}) copy-start(bf16[256,1152]{1,0:T(8,128)(2,1)} %get-tuple-element.19.packed) | copy-start | bytes 1769476
  53.5 36.8 %copy-start.2 = (bf16[1,512,256]{2,1,0:T(8,128)(2,1)S(1)}, bf16[1,512,256]{2,1,0:T(8,128)(2,1)}, u32[]{:S(2)}) copy-start(bf16[1,512,256]{2,1,0:T(8,128)(2,1)} %get-tuple-element.34) | copy-start | bytes 786436
  90.3 1.0 %copy-start.1 = (bf16[1,512,256]{2,1,0:T(8,128)(2,1)S(1)}, bf16[1,512,256]{2,1,0:T(8,128)(2,1)}, u32[]{:S(2)}) copy-start(bf16[1,512,256]{2,1,0:T(8,128)(2,1)} %get-tuple-element.35) | copy-start | bytes 786436

commit v2 on v1

v2 whole, which is shorter than its diff:
```python
import functools

import jax
import jax.numpy as jnp
from jax import lax
from jax.experimental import pallas as pl
from jax.experimental.pallas import tpu as pltpu
from jax.sharding import PartitionSpec as P

HEADS = 4
BALL = 128
LISTED = 4
BALLS = 8
ROWS = BALL * BALLS
HALF = ROWS // 2
D = 256
OWN = 128
EPSILON = 1e-06
XY = 16
MESH = pl.DeviceIdType.MESH
F32 = jnp.float32
BF16 = jnp.bfloat16


def dot(a, b):
    return jnp.dot(a, b, preferred_element_type=F32)


def dot_nt(a, b):
    return lax.dot_general(a, b, (((1,), (1,)), ((), ())), preferred_element_type=F32)


def rows_of(b, size=BALL):
    return pl.ds(pl.multiple_of(b * size, size), size)


def layers_kernel(
    near_count,
    planes,
    points,
    result_grad,
    lists_one,
    lists_two,
    rotation,
    gain_one,
    qkv_one,
    out_one,
    gain_two,
    qkv_two,
    out_two,
    result,
    points_grad,
    full_early,
    full_late,
    gain_sums,
    x_all,
    g_all,
    lists_v,
    lists_s,
    rot_v,
    w_own,
    w_out,
    normed_t,
    q_st,
    kv_all,
    k_t,
    v_t,
    att,
    mix_t,
    mixed,
    dqkv,
    parts,
    ngrad,
    perm,
    perm_t,
    early,
    late,
    near_early,
    near_late,
    deep_early,
    deep_late,
    near_gain,
    deep_gain,
    in_send,
    in_recv,
    own_sem,
    load_sem,
    smem_sem,
    mix_send,
    mix_recv,
    ng_send,
    ng_recv,
    send_xy,
    recv_xy,
    send_z,
    recv_z,
    send_all,
    recv_all,
    send_core,
    recv_core,
):
    c = lax.axis_index("pts")
    other = 1 - c
    geo = lax.axis_index("geo")
    z = geo // near_count
    xy = geo % near_count
    chunk = D // near_count
    gains = (gain_one, gain_two)
    qkvs = (qkv_one, qkv_two)
    outs = (out_one, out_two)

    def copy_to(device, src, dst, send, recv):
        return pltpu.make_async_remote_copy(
            src_ref=src,
            dst_ref=dst,
            send_sem=send,
            recv_sem=recv,
            device_id=device,
            device_id_type=MESH,
        )

    def remote(src, dst, send, recv):
        return copy_to({"pts": other}, src, dst, send, recv)

    def near(k):
        return {"geo": z * near_count + (xy + k) % near_count}

    def deep(k):
        return {"geo": ((z + k) % planes) * near_count + xy}

    barrier = pltpu.get_barrier_semaphore()
    pl.semaphore_signal(barrier, inc=1, device_id={"pts": other}, device_id_type=MESH)
    for k in range(1, near_count):
        pl.semaphore_signal(barrier, inc=1, device_id=near(k), device_id_type=MESH)
    for k in range(1, planes):
        pl.semaphore_signal(barrier, inc=1, device_id=deep(k), device_id_type=MESH)

    inputs = (
        (points.at[0], x_all.at[0, rows_of(c, HALF)]),
        (lists_one.at[0], lists_v.at[0, c]),
        (lists_two.at[0], lists_v.at[1, c]),
        (rotation, rot_v.at[c]),
        (result_grad.at[0], g_all.at[1, rows_of(c, HALF)]),
    )
    kept = [
        pltpu.make_async_copy(src, dst, own_sem.at[n]) for n, (src, dst) in enumerate(inputs)
    ]
    sent = [
        remote(src, dst, in_send.at[n], in_recv.at[n]) for n, (src, dst) in enumerate(inputs)
    ]
    loads = []
    for i in range(2):
        for n in range(3):
            part = pl.ds(pl.multiple_of(n * D + c * OWN, OWN), OWN)
            loads.append(
                pltpu.make_async_copy(
                    qkvs[i].at[:, part],
                    w_own.at[i, :, n * OWN : (n + 1) * OWN],
                    load_sem.at[4 * i + n],
                )
            )
        loads.append(pltpu.make_async_copy(outs[i], w_out.at[i], load_sem.at[4 * i + 3]))
    kept[0].start()
    for copy in loads[:3]:
        copy.start()
    for copy in kept[1:] + loads[3:]:
        copy.start()
    parts[LISTED * BALLS] = jnp.zeros((BALL, D), F32)
    col = pl.ds(pl.multiple_of(c * OWN, OWN), OWN)

    lane = lax.broadcasted_iota(jnp.int32, (BALL, OWN), 1)
    first = lane < OWN // 2

    def stacked(value):
        zero = jnp.zeros_like(value)
        return jnp.concatenate(
            [jnp.where(first, value, zero), jnp.where(first, zero, value)], axis=0
        )

    def unstacked_t(value):
        return jnp.concatenate([value[: OWN // 2, :BALL], value[OWN // 2 :, BALL:]], axis=0)

    def project(i, b):
        x = x_all[i, rows_of(b)].astype(F32)
        gain = gains[i][...].astype(F32).reshape(1, D)
        factor = lax.rsqrt(jnp.mean(x * x, axis=-1, keepdims=True) + EPSILON)
        normed = x * factor * gain
        normed_t[i, :, rows_of(b)] = normed.T.astype(BF16)
        qkv = dot(normed.astype(BF16), w_own[i])
        q = qkv[:, :OWN].astype(BF16).astype(F32) * 0.125
        q_st[i, b] = stacked(q).astype(BF16)
        kv_all[i, b] = qkv[:, OWN:].astype(BF16)
        k_t[i, b] = qkv[:, OWN : 2 * OWN].T.astype(BF16)
        v_t[i, b] = qkv[:, 2 * OWN :].T.astype(BF16)

    def listed(i, b):
        return [lists_s[i, b // 4, b % 4, n] for n in range(LISTED)]

    def attend(i, b):
        ids = listed(i, b)
        keys = jnp.concatenate([kv_all[i, t, :, :OWN] for t in ids], axis=0)
        scores = dot_nt(keys, q_st[i, b])
        top = jnp.max(scores, axis=0, keepdims=True)
        exponent = jnp.exp(scores - top)
        attention = exponent * (1.0 / jnp.sum(exponent, axis=0, keepdims=True))
        att[i, b] = attention
        values_t = jnp.concatenate([v_t[i, t] for t in ids], axis=1)
        own_t = unstacked_t(dot(values_t, attention.astype(BF16)))
        mix_t[i, :, rows_of(b)] = own_t.astype(BF16)
        mixed[i, c, rows_of(b)] = own_t.T.astype(BF16)

    def loop(count, body, unroll=4):
        lax.fori_loop(0, count, lambda j, _: body(j), None, unroll=unroll)

    def mix_copy(i, b, slot):
        ref = mixed.at[i, c, rows_of(b)]
        return remote(ref, ref, mix_send.at[i, slot], mix_recv.at[i, slot])

    def project_out(i, b):
        both = jnp.concatenate([mixed[i, 0, rows_of(b)], mixed[i, 1, rows_of(b)]], axis=1)
        x = x_all[i, rows_of(b)].astype(F32)
        return (x + dot(both, w_out[i])).astype(BF16)

    def build(b):
        here = rot_v[b // 4, :, rows_of(b % 4)].astype(F32)
        column = jnp.broadcast_to(here, (BALL, BALL)).T
        for n in range(BALLS):
            ids = (lane + n * BALL).astype(F32)
            perm[rows_of(b), n * BALL : (n + 1) * BALL] = jnp.where(
                ids == column, 1.0, 0.0
            ).astype(BF16)

    def build_t(b):
        ids = lax.broadcasted_iota(jnp.int32, (BALL, ROWS), 0) + b * BALL
        rot_row = jnp.concatenate([rot_v[0], rot_v[1]], axis=1)
        perm_t[rows_of(b)] = jnp.where(ids == rot_row, 1.0, 0.0).astype(BF16)

    kept[0].wait()
    for copy in loads[:3]:
        copy.wait()
    loop(4, lambda j: project(0, c * 4 + j))
    pl.semaphore_wait(barrier, near_count + planes - 1)
    for copy in sent:
        copy.start()
    for copy in kept[1:4]:
        copy.wait()
    loop(4, lambda j: build(c * 4 + j))
    for n in (1, 2, 3):
        sent[n].wait()
    to_smem = pltpu.make_async_copy(lists_v, lists_s, smem_sem)
    to_smem.start()
    sent[0].wait()
    loop(4, lambda j: project(0, other * 4 + j))
    to_smem.wait()
    for copy in loads[3:]:
        copy.wait()

    def attend_send(j):
        attend(0, j)
        mix_copy(0, j, j).start()

    loop(BALLS, attend_send)
    loop(BALLS, build_t)
    loop(4, lambda j: build(other * 4 + j))

    def hidden_rows(b):
        mix_copy(0, b, b).wait()
        x_all[2, rows_of(b)] = project_out(0, b)

    loop(BALLS, hidden_rows)
    x_all[1] = dot(perm[...], x_all[2]).astype(BF16)
    loop(BALLS, lambda b: project(1, b))

    def attend_two(j):
        attend(1, other * 4 + j)
        mix_copy(1, other * 4 + j, j).start()

    loop(4, attend_two)
    loop(4, lambda j: attend(1, c * 4 + j))

    def result_rows(j):
        mix_copy(1, other * 4 + j, j).wait()
        result[0, rows_of(j)] = project_out(1, c * 4 + j)

    loop(4, result_rows)
    kept[4].wait()
    sent[4].wait()

    def attend_back(i, b):
        ids = listed(i, b)
        mixed_grad = stacked(dot_nt(g_all[i, rows_of(b)], w_out[i, col, :])).astype(BF16)
        values = jnp.concatenate([kv_all[i, t, :, OWN:] for t in ids], axis=0)
        weights_grad = dot_nt(values, mixed_grad)
        attention = att[i, b]
        inner = jnp.sum(attention * weights_grad, axis=0, keepdims=True)
        scores_grad = (attention * (weights_grad - inner)).astype(BF16)
        values_grad = dot(attention.astype(BF16), mixed_grad)
        keys_grad = dot(scores_grad, q_st[i, b])
        for n in range(LISTED):
            parts[b * LISTED + n, :, :OWN] = keys_grad[n * BALL : (n + 1) * BALL]
            parts[b * LISTED + n, :, OWN:] = values_grad[n * BALL : (n + 1) * BALL]
        keys_t = jnp.concatenate([k_t[i, t] for t in ids], axis=1)
        query_grad_t = unstacked_t(dot(keys_t, scores_grad)) * 0.125
        dqkv[rows_of(b), :OWN] = query_grad_t.T.astype(BF16)

    def gather_parts(i, t):
        total = jnp.zeros((BALL, D), F32)
        for b in range(BALLS):
            at = jnp.int32(LISTED * BALLS)
            for n in range(LISTED):
                at = jnp.where(lists_s[i, b // 4, b % 4, n] == t, b * LISTED + n, at)
            total = total + parts[at]
        dqkv[rows_of(t), OWN:] = total.astype(BF16)

    def ng_copy(i, b, slot):
        ref = ngrad.at[i, c, rows_of(b)]
        return remote(ref, ref, ng_send.at[i, slot], ng_recv.at[i, slot])

    def partial_rows(i, b):
        ngrad[i, c, rows_of(b)] = dot_nt(dqkv[rows_of(b)], w_own[i]).astype(BF16)

    def row_grads(i, b):
        x = x_all[i, rows_of(b)].astype(F32)
        gain = gains[i][...].astype(F32).reshape(1, D)
        factor = lax.rsqrt(jnp.mean(x * x, axis=-1, keepdims=True) + EPSILON)
        grad = ngrad[i, 0, rows_of(b)].astype(F32) + ngrad[i, 1, rows_of(b)].astype(F32)
        grad = grad.astype(BF16).astype(F32)
        scaled = grad * gain
        inner = jnp.mean(scaled * x, axis=-1, keepdims=True)
        inputs_grad = factor * scaled - x * (factor * factor * factor) * inner
        rows = (g_all[i, rows_of(b)].astype(F32) + inputs_grad).astype(BF16)
        return rows, jnp.sum(grad * (x * factor), axis=0, keepdims=True)

    class Sum:
        def __init__(self, r, own, arrived, along, full):
            self.r, self.own, self.arrived, self.along, self.full = r, own, arrived, along, full
            at = rows_of(xy, chunk)
            self.first = [
                copy_to(
                    near(k),
                    own.at[rows_of((xy + k) % near_count, chunk)],
                    arrived.at[k - 1],
                    send_xy.at[r, k - 1],
                    recv_xy.at[r, k - 1],
                )
                for k in range(1, near_count)
            ]
            self.second = [
                copy_to(
                    deep(k), along.at[z], along.at[z], send_z.at[r, k - 1], recv_z.at[r, k - 1]
                )
                for k in range(1, planes)
            ]
            mine = full.at[c, at]
            self.third = [
                copy_to(near(k), mine, mine, send_all.at[r, k - 1], recv_all.at[r, k - 1])
                for k in range(1, near_count)
            ]
            pieces = [
                full.at[c, rows_of((xy - k + near_count) % near_count, chunk)]
                for k in range(near_count)
            ]
            self.across = [
                remote(piece, piece, send_core.at[r, k], recv_core.at[r, k])
                for k, piece in enumerate(pieces)
            ]

        def scatter(self):
            for copy in self.first:
                copy.start()

        def plane(self):
            total = self.own[rows_of(xy, chunk)].astype(F32)
            for k, copy in enumerate(self.first):
                copy.wait()
                total = total + self.arrived[k].astype(F32)
            self.along[z] = total.astype(BF16)
            for copy in self.second:
                copy.start()

        def column(self):
            for copy in self.second:
                copy.wait()
            total = self.along[0].astype(F32)
            for k in range(1, planes):
                total = total + self.along[k].astype(F32)
            self.full[c, rows_of(xy, chunk)] = total.astype(BF16)
            for copy in self.third:
                copy.start()
            self.across[0].start()

        def forward(self):
            for k, copy in enumerate(self.third):
                copy.wait_recv()
                self.across[k + 1].start()

        def finish(self):
            for copy in self.third:
                copy.wait_send()
            for copy in self.across:
                copy.wait()

    sum_early = Sum(0, early, near_early, deep_early, full_early)
    sum_late = Sum(1, late, near_late, deep_late, full_late)
    gain_first = [
        copy_to(
            near(k), near_gain.at[xy], near_gain.at[xy], send_xy.at[2, k - 1], recv_xy.at[2, k - 1]
        )
        for k in range(1, near_count)
    ]
    gain_second = [
        copy_to(deep(k), deep_gain.at[z], deep_gain.at[z], send_z.at[2, k - 1], recv_z.at[2, k - 1])
        for k in range(1, planes)
    ]
    gain_across = remote(
        gain_sums.at[c], gain_sums.at[c], send_core.at[2, 0], recv_core.at[2, 0]
    )

    loop(BALLS, lambda b: attend_back(1, b))
    loop(BALLS, lambda t: gather_parts(1, t))

    def partial_two(b):
        partial_rows(1, b)
        ng_copy(1, b, b).start()

    loop(BALLS, partial_two)
    early[:, : 3 * OWN] = dot(normed_t[1], dqkv[...]).astype(BF16)
    out_grad = dot(mix_t[1], g_all[1]).astype(BF16)
    early[:OWN, 3 * OWN : 4 * OWN] = out_grad[:, :OWN]
    early[OWN:, 3 * OWN : 4 * OWN] = out_grad[:, OWN:]

    def rows_two(b, total):
        ng_copy(1, b, b).wait()
        rows, gain_part = row_grads(1, b)
        x_all[2, rows_of(b)] = rows
        mine = ((b // 4) == c).astype(F32)
        return total + gain_part * mine

    gain_two_part = lax.fori_loop(0, BALLS, rows_two, jnp.zeros((1, D), F32), unroll=4)

    g_all[0] = dot(perm_t[...], x_all[2]).astype(BF16)
    out_grad = dot(mix_t[0], g_all[0]).astype(BF16)
    early[:OWN, 4 * OWN :] = out_grad[:, :OWN]
    early[OWN:, 4 * OWN :] = out_grad[:, OWN:]
    sum_early.scatter()
    loop(BALLS, lambda b: attend_back(0, b))
    loop(BALLS, lambda t: gather_parts(0, t))
    late[...] = dot(normed_t[0], dqkv[...]).astype(BF16)
    sum_late.scatter()

    def partial_one(j):
        partial_rows(0, other * 4 + j)
        ng_copy(0, other * 4 + j, j).start()

    loop(4, partial_one)
    loop(4, lambda j: partial_rows(0, c * 4 + j))
    sum_early.plane()

    def rows_one(j, total):
        ng_copy(0, other * 4 + j, j).wait()
        rows, gain_part = row_grads(0, c * 4 + j)
        points_grad[0, rows_of(j)] = rows
        return total + gain_part

    gain_one_part = lax.fori_loop(0, 4, rows_one, jnp.zeros((1, D), F32), unroll=4)
    near_gain[xy] = jnp.concatenate([gain_one_part, gain_two_part], axis=0)
    for copy in gain_first:
        copy.start()
    sum_late.plane()
    for copy in gain_first:
        copy.wait()
    deep_gain[z] = sum(near_gain[k] for k in range(near_count))
    for copy in gain_second:
        copy.start()
    sum_early.column()
    sum_late.column()
    for copy in gain_second:
        copy.wait()
    gain_sums[c] = sum(deep_gain[k] for k in range(planes))
    gain_across.start()
    sum_early.forward()
    sum_late.forward()
    sum_early.finish()
    sum_late.finish()
    gain_across.wait()


def spread_kernel(
    early,
    late,
    gain_sums,
    result_in,
    points_grad_in,
    result,
    points_grad,
    gain_one,
    qkv_one,
    out_one,
    gain_two,
    qkv_two,
    out_two,
):
    result[...] = result_in[...]
    points_grad[...] = points_grad_in[...]
    for core in range(2):
        here = slice(core * OWN, (core + 1) * OWN)
        for n in range(3):
            into = slice(n * D + core * OWN, n * D + (core + 1) * OWN)
            qkv_one[:, into] = late[core, :, n * OWN : (n + 1) * OWN].astype(F32)
            qkv_two[:, into] = early[core, :, n * OWN : (n + 1) * OWN].astype(F32)
        for at, out in ((4 * OWN, out_one), (3 * OWN, out_two)):
            out[here, :OWN] = early[core, :OWN, at : at + OWN].astype(F32)
            out[here, OWN:] = early[core, OWN:, at : at + OWN].astype(F32)
    gains = gain_sums[0] + gain_sums[1]
    gain_one[...] = gains[0]
    gain_two[...] = gains[1]


def vmem():
    return pl.BlockSpec(memory_space=pltpu.VMEM)


def hbm():
    return pl.BlockSpec(memory_space=pltpu.HBM)


def layers_call(near_count, planes, *args):
    chunk = D // near_count
    peers = max(near_count - 1, 1)
    deeper = max(planes - 1, 1)
    return pl.pallas_call(
        functools.partial(layers_kernel, near_count, planes),
        name="layers",
        out_shape=(
            jax.ShapeDtypeStruct((1, HALF, D), BF16),
            jax.ShapeDtypeStruct((1, HALF, D), BF16),
            jax.ShapeDtypeStruct((2, D, 5 * OWN), BF16),
            jax.ShapeDtypeStruct((2, D, 3 * OWN), BF16),
            jax.ShapeDtypeStruct((2, 2, D), F32),
        ),
        in_specs=[hbm()] * 5 + [vmem(), hbm(), hbm()] * 2,
        out_specs=(vmem(),) * 5,
        scratch_shapes=[
            pltpu.VMEM((3, ROWS, D), BF16),
            pltpu.VMEM((2, ROWS, D), BF16),
            pltpu.VMEM((2, 2, 4, LISTED), jnp.int32),
            pltpu.SMEM((2, 2, 4, LISTED), jnp.int32),
            pltpu.VMEM((2, 1, HALF), jnp.int32),
            pltpu.VMEM((2, D, 3 * OWN), BF16),
            pltpu.VMEM((2, D, D), BF16),
            pltpu.VMEM((2, D, ROWS), BF16),
            pltpu.VMEM((2, BALLS, 2 * BALL, OWN), BF16),
            pltpu.VMEM((2, BALLS, BALL, 2 * OWN), BF16),
            pltpu.VMEM((2, BALLS, OWN, BALL), BF16),
            pltpu.VMEM((2, BALLS, OWN, BALL), BF16),
            pltpu.VMEM((2, BALLS, LISTED * BALL, 2 * BALL), F32),
            pltpu.VMEM((2, OWN, ROWS), BF16),
            pltpu.VMEM((2, 2, ROWS, OWN), BF16),
            pltpu.VMEM((ROWS, 3 * OWN), BF16),
            pltpu.VMEM((LISTED * BALLS + 1, BALL, D), F32),
            pltpu.VMEM((2, 2, ROWS, D), BF16),
            pltpu.VMEM((ROWS, ROWS), BF16),
            pltpu.VMEM((ROWS, ROWS), BF16),
            pltpu.VMEM((D, 5 * OWN), BF16),
            pltpu.VMEM((D, 3 * OWN), BF16),
            pltpu.VMEM((peers, chunk, 5 * OWN), BF16),
            pltpu.VMEM((peers, chunk, 3 * OWN), BF16),
            pltpu.VMEM((planes, chunk, 5 * OWN), BF16),
            pltpu.VMEM((planes, chunk, 3 * OWN), BF16),
            pltpu.VMEM((near_count, 2, D), F32),
            pltpu.VMEM((planes, 2, D), F32),
            pltpu.SemaphoreType.DMA((5,)),
            pltpu.SemaphoreType.DMA((5,)),
            pltpu.SemaphoreType.DMA((5,)),
            pltpu.SemaphoreType.DMA((8,)),
            pltpu.SemaphoreType.DMA,
            pltpu.SemaphoreType.DMA((2, BALLS)),
            pltpu.SemaphoreType.DMA((2, BALLS)),
            pltpu.SemaphoreType.DMA((2, BALLS)),
            pltpu.SemaphoreType.DMA((2, BALLS)),
            pltpu.SemaphoreType.DMA((3, peers)),
            pltpu.SemaphoreType.DMA((3, peers)),
            pltpu.SemaphoreType.DMA((3, deeper)),
            pltpu.SemaphoreType.DMA((3, deeper)),
            pltpu.SemaphoreType.DMA((2, peers)),
            pltpu.SemaphoreType.DMA((2, peers)),
            pltpu.SemaphoreType.DMA((3, near_count)),
            pltpu.SemaphoreType.DMA((3, near_count)),
        ],
        compiler_params=pltpu.CompilerParams(
            collective_id=0, has_side_effects=True, vmem_limit_bytes=56 << 20
        ),
    )(*args)


def spread_call(early, late, gain_sums, result, points_grad):
    shapes = (
        jax.ShapeDtypeStruct((D,), F32),
        jax.ShapeDtypeStruct((D, 3 * D), F32),
        jax.ShapeDtypeStruct((D, D), F32),
    )
    rows = jax.ShapeDtypeStruct((1, HALF, D), BF16)
    return pl.pallas_call(
        spread_kernel,
        name="spread",
        out_shape=(rows, rows) + shapes + shapes,
        in_specs=[vmem()] * 5,
        out_specs=(vmem(),) * 8,
    )(early, late, gain_sums, result, points_grad)


def local(*args):
    planes = lax.axis_size("geo") // XY
    result, points_grad, early, late, gain_sums = layers_call(XY, planes, *args)
    return spread_call(early, late, gain_sums, result, points_grad)


def solution(mesh):
    rows = P("geo", "pts", None)
    placed = (rows, rows, rows, rows, P("geo", "pts"), P(), P(), P(), P(), P(), P())
    return jax.shard_map(
        local,
        mesh=mesh,
        in_specs=placed,
        out_specs=(rows, rows, P(), P(), P(), P(), P(), P()),
        check_vma=False,
    )
```

time: 96.5 us -> 72 us (0.75)
  Pallas kernels: 86.7 us -> 71.3 us
  local copies, waits for them, and re-layouts: 8.88 us -> 0 us
    pallas_call x2, Pallas kernels: 86.7 us -> 71.3 us  [the longest x1 68.4 us: layers_call(): pl.pallas_call(functools.partial(layers_kernel, near_count, planes), name...]
    unnamed x16 -> x0, local copies, waits for them, and re-layouts: 7.09 us -> none
    reshape x2 -> x0, local copies, waits for them, and re-layouts: 1.79 us -> none  [the longest x1 1.23 us: local(): gain_one.reshape(1, D)]
where the time goes in v2:
time: 72 us; the launch traced here: 71.9 us
  Pallas kernels  71.3 us (99%)
    pallas_call x1, Pallas kernels, layers_call(): pl.pallas_call(functools.partial(layers_kernel, near_count, planes), name...  68.4 us
    pallas_call x1, Pallas kernels, spread_call(): pl.pallas_call(spread_kernel, name='spread', out_shape=(rows, rows) + sha...  2.86 us

profile of v2, /device:TPU:1, one launch (start us, length us, event | category | flops | bytes accessed | tf_op | source)
XLA Modules:
  0.0 71.9 jit_solution(6488243469592600287)
XLA Ops:
  0.6 68.4 %layers.1 = (bf16[1,512,256]{2,1,0:T(8,128)(2,1)}, bf16[1,512,256]{2,1,0:T(8,128)(2,1)}, bf16[2,256,640]{2,1,0:T(8,128)(2,1)}, bf16[2,256,384]{2,1,0:T(8,128)(2,1)}, f32[2,2,256]{2,1,0:T(2,128)}) custom-call(bf16[1,512,256]{2,1,0:T(8,128)(2,1)} %points.1, bf16[1,512,256]{2,1,0:T(8,128)(2,1)} %result_grad.1, s32[1,4,4]{2,1,0:T(4,128)} %lists_one.1, ...), custom_call_target="tpu_custom_call" | custom-call | tf_op jit(solution)/shard_map/layers/pallas_call | solution.py:531
  69.0 2.9 %spread.1 = (bf16[1,512,256]{2,1,0:T(8,128)(2,1)}, bf16[1,512,256]{2,1,0:T(8,128)(2,1)}, f32[256]{0:T(256)}, f32[256,768]{1,0:T(8,128)}, f32[256,256]{1,0:T(8,12...) custom-call(bf16[2,256,640]{2,1,0:T(8,128)(2,1)} %get-tuple-element.13.early, ...), custom_call_target="tpu_custom_call" | custom-call | tf_op jit(solution)/shard_map/spread/pallas_call | solution.py:603

commit v3 on v2

--- a/solution.py
+++ b/solution.py
@@ -51,6 +51,7 @@
     result,
     points_grad,
     full_early,
+    full_third,
     full_late,
     gain_sums,
     x_all,
@@ -67,6 +68,7 @@
     v_t,
     att,
     mix_t,
+    mix_f,
     mixed,
     dqkv,
     parts,
@@ -74,10 +76,13 @@
     perm,
     perm_t,
     early,
+    third,
     late,
     near_early,
+    near_third,
     near_late,
     deep_early,
+    deep_third,
     deep_late,
     near_gain,
     deep_gain,
@@ -198,14 +203,19 @@
 
     def attend(i, b):
         ids = listed(i, b)
-        keys = jnp.concatenate([kv_all[i, t, :, :OWN] for t in ids], axis=0)
-        scores = dot_nt(keys, q_st[i, b])
-        top = jnp.max(scores, axis=0, keepdims=True)
-        exponent = jnp.exp(scores - top)
-        attention = exponent * (1.0 / jnp.sum(exponent, axis=0, keepdims=True))
-        att[i, b] = attention
+        queries = q_st[i, b]
+        scores = [dot_nt(kv_all[i, t, :, :OWN], queries) for t in ids]
+        top = jnp.maximum(jnp.maximum(scores[0], scores[1]), jnp.maximum(scores[2], scores[3]))
+        top = jnp.max(top, axis=0, keepdims=True)
+        exponents = [jnp.exp(score - top) for score in scores]
+        total = (exponents[0] + exponents[1]) + (exponents[2] + exponents[3])
+        scale = 1.0 / jnp.sum(total, axis=0, keepdims=True)
+        weights = [(exponent * scale).astype(BF16) for exponent in exponents]
+        for n in range(LISTED):
+            att[i, b, n * BALL : (n + 1) * BALL] = weights[n]
         values_t = jnp.concatenate([v_t[i, t] for t in ids], axis=1)
-        own_t = unstacked_t(dot(values_t, attention.astype(BF16)))
+        own_t = unstacked_t(dot(values_t, jnp.concatenate(weights, axis=0)))
+        mix_f[i, :, rows_of(b)] = own_t
         mix_t[i, :, rows_of(b)] = own_t.astype(BF16)
         mixed[i, c, rows_of(b)] = own_t.T.astype(BF16)
 
@@ -239,12 +249,12 @@
     for copy in loads[:3]:
         copy.wait()
     loop(4, lambda j: project(0, c * 4 + j))
+    for copy in kept[1:4]:
+        copy.wait()
+    loop(4, lambda j: build(c * 4 + j))
     pl.semaphore_wait(barrier, near_count + planes - 1)
     for copy in sent:
         copy.start()
-    for copy in kept[1:4]:
-        copy.wait()
-    loop(4, lambda j: build(c * 4 + j))
     for n in (1, 2, 3):
         sent[n].wait()
     to_smem = pltpu.make_async_copy(lists_v, lists_s, smem_sem)
@@ -282,19 +292,37 @@
         mix_copy(1, other * 4 + j, j).wait()
         result[0, rows_of(j)] = project_out(1, c * 4 + j)
 
-    loop(4, result_rows)
     kept[4].wait()
     sent[4].wait()
 
     def attend_back(i, b):
         ids = listed(i, b)
-        mixed_grad = stacked(dot_nt(g_all[i, rows_of(b)], w_out[i, col, :])).astype(BF16)
+        grads = g_all[i, rows_of(b)]
+        own_out = w_out[i, col, :]
+        mixed_grad = stacked(dot_nt(grads, own_out)).astype(BF16)
+        mixed_grad_t = dot_nt(own_out, grads).astype(BF16).astype(F32)
+        product = mixed_grad_t * mix_f[i, :, rows_of(b)]
+        half = OWN // 2
+        inner = jnp.concatenate(
+            [
+                jnp.sum(product[:half], axis=0, keepdims=True),
+                jnp.sum(product[half:], axis=0, keepdims=True),
+            ],
+            axis=1,
+        )
         values = jnp.concatenate([kv_all[i, t, :, OWN:] for t in ids], axis=0)
-        weights_grad = dot_nt(values, mixed_grad)
-        attention = att[i, b]
-        inner = jnp.sum(attention * weights_grad, axis=0, keepdims=True)
-        scores_grad = (attention * (weights_grad - inner)).astype(BF16)
-        values_grad = dot(attention.astype(BF16), mixed_grad)
+        weights = att[i, b]
+        scores_grad = jnp.concatenate(
+            [
+                (
+                    weights[:, cols].astype(F32)
+                    * (dot_nt(values, mixed_grad[cols]) - inner[:, cols])
+                ).astype(BF16)
+                for cols in (slice(0, BALL), slice(BALL, 2 * BALL))
+            ],
+            axis=1,
+        )
+        values_grad = dot(weights, mixed_grad)
         keys_grad = dot(scores_grad, q_st[i, b])
         for n in range(LISTED):
             parts[b * LISTED + n, :, :OWN] = keys_grad[n * BALL : (n + 1) * BALL]
@@ -332,18 +360,21 @@
         return rows, jnp.sum(grad * (x * factor), axis=0, keepdims=True)
 
     class Sum:
-        def __init__(self, r, own, arrived, along, full):
+        def __init__(self, r, groups, own, arrived, along, full):
             self.r, self.own, self.arrived, self.along, self.full = r, own, arrived, along, full
             at = rows_of(xy, chunk)
             self.first = [
-                copy_to(
-                    near(k),
-                    own.at[rows_of((xy + k) % near_count, chunk)],
-                    arrived.at[k - 1],
-                    send_xy.at[r, k - 1],
-                    recv_xy.at[r, k - 1],
-                )
-                for k in range(1, near_count)
+                [
+                    copy_to(
+                        near(k),
+                        own.at[rows_of((xy + k) % near_count, chunk), cols],
+                        arrived.at[k - 1, :, cols],
+                        send_xy.at[r + m, k - 1],
+                        recv_xy.at[r + m, k - 1],
+                    )
+                    for k in range(1, near_count)
+                ]
+                for m, cols in enumerate(groups)
             ]
             self.second = [
                 copy_to(
@@ -365,14 +396,15 @@
                 for k, piece in enumerate(pieces)
             ]
 
-        def scatter(self):
-            for copy in self.first:
+        def scatter(self, m=0):
+            for copy in self.first[m]:
                 copy.start()
 
         def plane(self):
             total = self.own[rows_of(xy, chunk)].astype(F32)
-            for k, copy in enumerate(self.first):
-                copy.wait()
+            for k in range(near_count - 1):
+                for group in self.first:
+                    group[k].wait()
                 total = total + self.arrived[k].astype(F32)
             self.along[z] = total.astype(BF16)
             for copy in self.second:
@@ -400,22 +432,31 @@
             for copy in self.across:
                 copy.wait()
 
-    sum_early = Sum(0, early, near_early, deep_early, full_early)
-    sum_late = Sum(1, late, near_late, deep_late, full_late)
+    out_cols, in_cols = slice(3 * OWN, 4 * OWN), slice(0, 3 * OWN)
+    sum_early = Sum(0, (out_cols, in_cols), early, near_early, deep_early, full_early)
+    sum_third = Sum(2, (slice(0, OWN),), third, near_third, deep_third, full_third)
+    sum_late = Sum(3, (in_cols,), late, near_late, deep_late, full_late)
     gain_first = [
         copy_to(
-            near(k), near_gain.at[xy], near_gain.at[xy], send_xy.at[2, k - 1], recv_xy.at[2, k - 1]
+            near(k), near_gain.at[xy], near_gain.at[xy], send_xy.at[4, k - 1], recv_xy.at[4, k - 1]
         )
         for k in range(1, near_count)
     ]
     gain_second = [
-        copy_to(deep(k), deep_gain.at[z], deep_gain.at[z], send_z.at[2, k - 1], recv_z.at[2, k - 1])
+        copy_to(deep(k), deep_gain.at[z], deep_gain.at[z], send_z.at[4, k - 1], recv_z.at[4, k - 1])
         for k in range(1, planes)
     ]
     gain_across = remote(
-        gain_sums.at[c], gain_sums.at[c], send_core.at[2, 0], recv_core.at[2, 0]
+        gain_sums.at[c], gain_sums.at[c], send_core.at[4, 0], recv_core.at[4, 0]
     )
 
+    def pack_out(i, into, at):
+        out_grad = dot(mix_t[i], g_all[i]).astype(BF16)
+        into[:OWN, at : at + OWN] = out_grad[:, :OWN]
+        into[OWN:, at : at + OWN] = out_grad[:, OWN:]
+
+    pack_out(1, early, 3 * OWN)
+    sum_early.scatter(0)
     loop(BALLS, lambda b: attend_back(1, b))
     loop(BALLS, lambda t: gather_parts(1, t))
 
@@ -425,9 +466,7 @@
 
     loop(BALLS, partial_two)
     early[:, : 3 * OWN] = dot(normed_t[1], dqkv[...]).astype(BF16)
-    out_grad = dot(mix_t[1], g_all[1]).astype(BF16)
-    early[:OWN, 3 * OWN : 4 * OWN] = out_grad[:, :OWN]
-    early[OWN:, 3 * OWN : 4 * OWN] = out_grad[:, OWN:]
+    sum_early.scatter(1)
 
     def rows_two(b, total):
         ng_copy(1, b, b).wait()
@@ -439,14 +478,15 @@
     gain_two_part = lax.fori_loop(0, BALLS, rows_two, jnp.zeros((1, D), F32), unroll=4)
 
     g_all[0] = dot(perm_t[...], x_all[2]).astype(BF16)
-    out_grad = dot(mix_t[0], g_all[0]).astype(BF16)
-    early[:OWN, 4 * OWN :] = out_grad[:, :OWN]
-    early[OWN:, 4 * OWN :] = out_grad[:, OWN:]
-    sum_early.scatter()
-    loop(BALLS, lambda b: attend_back(0, b))
+    pack_out(0, third, 0)
+    sum_third.scatter()
+    loop(4, lambda b: attend_back(0, b))
+    sum_early.plane()
+    loop(4, lambda b: attend_back(0, b + 4))
     loop(BALLS, lambda t: gather_parts(0, t))
     late[...] = dot(normed_t[0], dqkv[...]).astype(BF16)
     sum_late.scatter()
+    sum_third.plane()
 
     def partial_one(j):
         partial_rows(0, other * 4 + j)
@@ -454,7 +494,6 @@
 
     loop(4, partial_one)
     loop(4, lambda j: partial_rows(0, c * 4 + j))
-    sum_early.plane()
 
     def rows_one(j, total):
         ng_copy(0, other * 4 + j, j).wait()
@@ -466,27 +505,31 @@
     near_gain[xy] = jnp.concatenate([gain_one_part, gain_two_part], axis=0)
     for copy in gain_first:
         copy.start()
+    sum_early.column()
     sum_late.plane()
+    sum_third.column()
     for copy in gain_first:
         copy.wait()
     deep_gain[z] = sum(near_gain[k] for k in range(near_count))
     for copy in gain_second:
         copy.start()
-    sum_early.column()
+    loop(4, result_rows)
     sum_late.column()
     for copy in gain_second:
         copy.wait()
     gain_sums[c] = sum(deep_gain[k] for k in range(planes))
     gain_across.start()
-    sum_early.forward()
-    sum_late.forward()
-    sum_early.finish()
-    sum_late.finish()
+    sums = (sum_early, sum_third, sum_late)
+    for item in sums:
+        item.forward()
+    for item in sums:
+        item.finish()
     gain_across.wait()
 
 
 def spread_kernel(
     early,
+    third,
     late,
     gain_sums,
     result_in,
@@ -508,9 +551,9 @@
             into = slice(n * D + core * OWN, n * D + (core + 1) * OWN)
             qkv_one[:, into] = late[core, :, n * OWN : (n + 1) * OWN].astype(F32)
             qkv_two[:, into] = early[core, :, n * OWN : (n + 1) * OWN].astype(F32)
-        for at, out in ((4 * OWN, out_one), (3 * OWN, out_two)):
-            out[here, :OWN] = early[core, :OWN, at : at + OWN].astype(F32)
-            out[here, OWN:] = early[core, OWN:, at : at + OWN].astype(F32)
+        for at, of, out in ((0, third, out_one), (3 * OWN, early, out_two)):
+            out[here, :OWN] = of[core, :OWN, at : at + OWN].astype(F32)
+            out[here, OWN:] = of[core, OWN:, at : at + OWN].astype(F32)
     gains = gain_sums[0] + gain_sums[1]
     gain_one[...] = gains[0]
     gain_two[...] = gains[1]
@@ -534,12 +577,13 @@
         out_shape=(
             jax.ShapeDtypeStruct((1, HALF, D), BF16),
             jax.ShapeDtypeStruct((1, HALF, D), BF16),
-            jax.ShapeDtypeStruct((2, D, 5 * OWN), BF16),
+            jax.ShapeDtypeStruct((2, D, 4 * OWN), BF16),
+            jax.ShapeDtypeStruct((2, D, OWN), BF16),
             jax.ShapeDtypeStruct((2, D, 3 * OWN), BF16),
             jax.ShapeDtypeStruct((2, 2, D), F32),
         ),
         in_specs=[hbm()] * 5 + [vmem(), hbm(), hbm()] * 2,
-        out_specs=(vmem(),) * 5,
+        out_specs=(vmem(),) * 6,
         scratch_shapes=[
             pltpu.VMEM((3, ROWS, D), BF16),
             pltpu.VMEM((2, ROWS, D), BF16),
@@ -553,19 +597,23 @@
             pltpu.VMEM((2, BALLS, BALL, 2 * OWN), BF16),
             pltpu.VMEM((2, BALLS, OWN, BALL), BF16),
             pltpu.VMEM((2, BALLS, OWN, BALL), BF16),
-            pltpu.VMEM((2, BALLS, LISTED * BALL, 2 * BALL), F32),
+            pltpu.VMEM((2, BALLS, LISTED * BALL, 2 * BALL), BF16),
             pltpu.VMEM((2, OWN, ROWS), BF16),
+            pltpu.VMEM((2, OWN, ROWS), F32),
             pltpu.VMEM((2, 2, ROWS, OWN), BF16),
             pltpu.VMEM((ROWS, 3 * OWN), BF16),
             pltpu.VMEM((LISTED * BALLS + 1, BALL, D), F32),
             pltpu.VMEM((2, 2, ROWS, D), BF16),
             pltpu.VMEM((ROWS, ROWS), BF16),
             pltpu.VMEM((ROWS, ROWS), BF16),
-            pltpu.VMEM((D, 5 * OWN), BF16),
+            pltpu.VMEM((D, 4 * OWN), BF16),
+            pltpu.VMEM((D, OWN), BF16),
             pltpu.VMEM((D, 3 * OWN), BF16),
-            pltpu.VMEM((peers, chunk, 5 * OWN), BF16),
+            pltpu.VMEM((peers, chunk, 4 * OWN), BF16),
+            pltpu.VMEM((peers, chunk, OWN), BF16),
             pltpu.VMEM((peers, chunk, 3 * OWN), BF16),
-            pltpu.VMEM((planes, chunk, 5 * OWN), BF16),
+            pltpu.VMEM((planes, chunk, 4 * OWN), BF16),
+            pltpu.VMEM((planes, chunk, OWN), BF16),
             pltpu.VMEM((planes, chunk, 3 * OWN), BF16),
             pltpu.VMEM((near_count, 2, D), F32),
             pltpu.VMEM((planes, 2, D), F32),
@@ -578,14 +626,14 @@
             pltpu.SemaphoreType.DMA((2, BALLS)),
             pltpu.SemaphoreType.DMA((2, BALLS)),
             pltpu.SemaphoreType.DMA((2, BALLS)),
-            pltpu.SemaphoreType.DMA((3, peers)),
-            pltpu.SemaphoreType.DMA((3, peers)),
-            pltpu.SemaphoreType.DMA((3, deeper)),
-            pltpu.SemaphoreType.DMA((3, deeper)),
-            pltpu.SemaphoreType.DMA((2, peers)),
-            pltpu.SemaphoreType.DMA((2, peers)),
-            pltpu.SemaphoreType.DMA((3, near_count)),
-            pltpu.SemaphoreType.DMA((3, near_count)),
+            pltpu.SemaphoreType.DMA((5, peers)),
+            pltpu.SemaphoreType.DMA((5, peers)),
+            pltpu.SemaphoreType.DMA((5, deeper)),
+            pltpu.SemaphoreType.DMA((5, deeper)),
+            pltpu.SemaphoreType.DMA((4, peers)),
+            pltpu.SemaphoreType.DMA((4, peers)),
+            pltpu.SemaphoreType.DMA((5, near_count)),
+            pltpu.SemaphoreType.DMA((5, near_count)),
         ],
         compiler_params=pltpu.CompilerParams(
             collective_id=0, has_side_effects=True, vmem_limit_bytes=56 << 20
@@ -593,7 +641,7 @@
     )(*args)
 
 
-def spread_call(early, late, gain_sums, result, points_grad):
+def spread_call(*args):
     shapes = (
         jax.ShapeDtypeStruct((D,), F32),
         jax.ShapeDtypeStruct((D, 3 * D), F32),
@@ -604,15 +652,16 @@
         spread_kernel,
         name="spread",
         out_shape=(rows, rows) + shapes + shapes,
-        in_specs=[vmem()] * 5,
+        in_specs=[vmem()] * 6,
         out_specs=(vmem(),) * 8,
-    )(early, late, gain_sums, result, points_grad)
+        compiler_params=pltpu.CompilerParams(vmem_limit_bytes=16 << 20),
+    )(*args)
 
 
 def local(*args):
     planes = lax.axis_size("geo") // XY
-    result, points_grad, early, late, gain_sums = layers_call(XY, planes, *args)
-    return spread_call(early, late, gain_sums, result, points_grad)
+    result, points_grad, *sums = layers_call(XY, planes, *args)
+    return spread_call(*sums, result, points_grad)
 
 
 def solution(mesh):

time: 72 us -> 74.8 us (1.039)
  local copies, waits for them, and re-layouts: 0 us -> 5.51 us
  Pallas kernels: 71.3 us -> 68.4 us
    unnamed x0 -> x12, local copies, waits for them, and re-layouts: none -> 5.51 us
    pallas_call x1, Pallas kernels: 68.4 us -> 66.7 us  [layers_call(): pl.pallas_call(functools.partial(layers_kernel, near_count, planes), name...]
    pallas_call x1, Pallas kernels: 2.86 us -> 1.63 us  [spread_call(): pl.pallas_call(spread_kernel, name='spread', out_shape=(rows, rows) + sha...]
where the time goes in v3:
time: 74.8 us; the launch traced here: 74.5 us
  Pallas kernels  68.4 us (91%)
  local copies, waits for them, and re-layouts  5.51 us (7%)
    pallas_call x1, Pallas kernels, layers_call(): pl.pallas_call(functools.partial(layers_kernel, near_count, planes), name...  66.7 us
    unnamed x12, local copies, waits for them, and re-layouts  5.51 us
    pallas_call x1, Pallas kernels, spread_call(): pl.pallas_call(spread_kernel, name='spread', out_shape=(rows, rows) + sha...  1.63 us

profile of v3, /device:TPU:1, one launch (start us, length us, event | category | flops | bytes accessed | tf_op | source)
XLA Modules:
  0.0 74.5 jit_solution(5321249838997534599)
XLA Ops:
  0.6 66.7 %layers.1 = (bf16[1,512,256]{2,1,0:T(8,128)(2,1)}, bf16[1,512,256]{2,1,0:T(8,128)(2,1)}, bf16[2,256,512]{2,1,0:T(8,128)(2,1)}, bf16[2,256,128]{2,1,0:T(8,128)(2,...) custom-call(bf16[1,512,256]{2,1,0:T(8,128)(2,1)} %points.1, bf16[1,512,256]{2,1,0:T(8,128)(2,1)} %result_grad.1, ...), custom_call_target="tpu_custom_call" | custom-call | tf_op jit(solution)/shard_map/layers/pallas_call | solution.py:574
  67.4 0.0 copy-start.5
  67.4 0.7 copy-done.5
  68.1 0.0 copy-start
  68.1 1.0 %copy-done = bf16[2,256,512]{2,1,0:T(8,128)(2,1)S(1)} copy-done((bf16[2,256,512]{2,1,0:T(8,128)(2,1)S(1)}, bf16[2,256,512]{2,1,0:T(8,128)(2,1)}, u32[]{:S(2)}) %copy-start) | copy-done | bytes 524312
  69.1 0.0 copy-start.1
  69.1 1.0 %copy-done.1 = bf16[2,256,384]{2,1,0:T(8,128)(2,1)S(1)} copy-done((bf16[2,256,384]{2,1,0:T(8,128)(2,1)S(1)}, bf16[2,256,384]{2,1,0:T(8,128)(2,1)}, u32[]{:S(2)}) %copy-start.1) | copy-done | bytes 393240
  70.1 0.0 copy-start.2
  70.1 0.9 %copy-done.2 = bf16[1,512,256]{2,1,0:T(8,128)(2,1)S(1)} copy-done((bf16[1,512,256]{2,1,0:T(8,128)(2,1)S(1)}, bf16[1,512,256]{2,1,0:T(8,128)(2,1)}, u32[]{:S(2)}) %copy-start.2) | copy-done | bytes 262168
  71.0 0.0 copy-start.3
  71.1 0.9 %copy-done.3 = bf16[1,512,256]{2,1,0:T(8,128)(2,1)S(1)} copy-done((bf16[1,512,256]{2,1,0:T(8,128)(2,1)S(1)}, bf16[1,512,256]{2,1,0:T(8,128)(2,1)}, u32[]{:S(2)}) %copy-start.3) | copy-done | bytes 262168
  72.0 0.0 copy-start.4
  72.0 0.9 %copy-done.4 = bf16[2,256,128]{2,1,0:T(8,128)(2,1)S(1)} copy-done((bf16[2,256,128]{2,1,0:T(8,128)(2,1)S(1)}, bf16[2,256,128]{2,1,0:T(8,128)(2,1)}, u32[]{:S(2)}) %copy-start.4) | copy-done | bytes 131096
  72.9 1.6 %spread.1 = (bf16[1,512,256]{2,1,0:T(8,128)(2,1)}, bf16[1,512,256]{2,1,0:T(8,128)(2,1)}, f32[256]{0:T(256)}, f32[256,768]{1,0:T(8,128)}, f32[256,256]{1,0:T(8,12...) custom-call(bf16[2,256,512]{2,1,0:T(8,128)(2,1)S(1)} %copy-done, bf16[2,256,128]{2,1,0:T(8,128)(2,1)S(1)} %copy-done.4, ...), custom_call_target="tpu_custom_call" | custom-call | tf_op jit(solution)/shard_map/spread/pallas_call | solution.py:651
Async XLA Ops:
  67.4 0.7 copy-start.5
  68.1 1.0 %copy-start = (bf16[2,256,512]{2,1,0:T(8,128)(2,1)S(1)}, bf16[2,256,512]{2,1,0:T(8,128)(2,1)}, u32[]{:S(2)}) copy-start(bf16[2,256,512]{2,1,0:T(8,128)(2,1)} %get-tuple-element.14.early) | copy-start | bytes 1572868
  69.1 1.0 %copy-start.1 = (bf16[2,256,384]{2,1,0:T(8,128)(2,1)S(1)}, bf16[2,256,384]{2,1,0:T(8,128)(2,1)}, u32[]{:S(2)}) copy-start(bf16[2,256,384]{2,1,0:T(8,128)(2,1)} %get-tuple-element.16.late) | copy-start | bytes 1179652
  70.1 0.9 %copy-start.2 = (bf16[1,512,256]{2,1,0:T(8,128)(2,1)S(1)}, bf16[1,512,256]{2,1,0:T(8,128)(2,1)}, u32[]{:S(2)}) copy-start(bf16[1,512,256]{2,1,0:T(8,128)(2,1)} %get-tuple-element.18.result_in) | copy-start | bytes 786436
  71.0 0.9 %copy-start.3 = (bf16[1,512,256]{2,1,0:T(8,128)(2,1)S(1)}, bf16[1,512,256]{2,1,0:T(8,128)(2,1)}, u32[]{:S(2)}) copy-start(bf16[1,512,256]{2,1,0:T(8,128)(2,1)} %get-tuple-element.19.points_grad_in) | copy-start | bytes 786436
  72.0 0.9 %copy-start.4 = (bf16[2,256,128]{2,1,0:T(8,128)(2,1)S(1)}, bf16[2,256,128]{2,1,0:T(8,128)(2,1)}, u32[]{:S(2)}) copy-start(bf16[2,256,128]{2,1,0:T(8,128)(2,1)} %get-tuple-element.15.third) | copy-start | bytes 393220

commit v4 on v2

--- a/solution.py
+++ b/solution.py
@@ -67,6 +67,7 @@
     v_t,
     att,
     mix_t,
+    mix_f,
     mixed,
     dqkv,
     parts,
@@ -198,14 +199,19 @@
 
     def attend(i, b):
         ids = listed(i, b)
-        keys = jnp.concatenate([kv_all[i, t, :, :OWN] for t in ids], axis=0)
-        scores = dot_nt(keys, q_st[i, b])
-        top = jnp.max(scores, axis=0, keepdims=True)
-        exponent = jnp.exp(scores - top)
-        attention = exponent * (1.0 / jnp.sum(exponent, axis=0, keepdims=True))
-        att[i, b] = attention
+        queries = q_st[i, b]
+        scores = [dot_nt(kv_all[i, t, :, :OWN], queries) for t in ids]
+        top = jnp.maximum(jnp.maximum(scores[0], scores[1]), jnp.maximum(scores[2], scores[3]))
+        top = jnp.max(top, axis=0, keepdims=True)
+        exponents = [jnp.exp(score - top) for score in scores]
+        total = (exponents[0] + exponents[1]) + (exponents[2] + exponents[3])
+        scale = 1.0 / jnp.sum(total, axis=0, keepdims=True)
+        weights = [(exponent * scale).astype(BF16) for exponent in exponents]
+        for n in range(LISTED):
+            att[i, b, n * BALL : (n + 1) * BALL] = weights[n]
         values_t = jnp.concatenate([v_t[i, t] for t in ids], axis=1)
-        own_t = unstacked_t(dot(values_t, attention.astype(BF16)))
+        own_t = unstacked_t(dot(values_t, jnp.concatenate(weights, axis=0)))
+        mix_f[i, :, rows_of(b)] = own_t
         mix_t[i, :, rows_of(b)] = own_t.astype(BF16)
         mixed[i, c, rows_of(b)] = own_t.T.astype(BF16)
 
@@ -239,12 +245,12 @@
     for copy in loads[:3]:
         copy.wait()
     loop(4, lambda j: project(0, c * 4 + j))
+    for copy in kept[1:4]:
+        copy.wait()
+    loop(4, lambda j: build(c * 4 + j))
     pl.semaphore_wait(barrier, near_count + planes - 1)
     for copy in sent:
         copy.start()
-    for copy in kept[1:4]:
-        copy.wait()
-    loop(4, lambda j: build(c * 4 + j))
     for n in (1, 2, 3):
         sent[n].wait()
     to_smem = pltpu.make_async_copy(lists_v, lists_s, smem_sem)
@@ -282,19 +288,37 @@
         mix_copy(1, other * 4 + j, j).wait()
         result[0, rows_of(j)] = project_out(1, c * 4 + j)
 
-    loop(4, result_rows)
     kept[4].wait()
     sent[4].wait()
 
     def attend_back(i, b):
         ids = listed(i, b)
-        mixed_grad = stacked(dot_nt(g_all[i, rows_of(b)], w_out[i, col, :])).astype(BF16)
+        grads = g_all[i, rows_of(b)]
+        own_out = w_out[i, col, :]
+        mixed_grad = stacked(dot_nt(grads, own_out)).astype(BF16)
+        mixed_grad_t = dot_nt(own_out, grads).astype(BF16).astype(F32)
+        product = mixed_grad_t * mix_f[i, :, rows_of(b)]
+        half = OWN // 2
+        inner = jnp.concatenate(
+            [
+                jnp.sum(product[:half], axis=0, keepdims=True),
+                jnp.sum(product[half:], axis=0, keepdims=True),
+            ],
+            axis=1,
+        )
         values = jnp.concatenate([kv_all[i, t, :, OWN:] for t in ids], axis=0)
-        weights_grad = dot_nt(values, mixed_grad)
-        attention = att[i, b]
-        inner = jnp.sum(attention * weights_grad, axis=0, keepdims=True)
-        scores_grad = (attention * (weights_grad - inner)).astype(BF16)
-        values_grad = dot(attention.astype(BF16), mixed_grad)
+        weights = att[i, b]
+        scores_grad = jnp.concatenate(
+            [
+                (
+                    weights[:, cols].astype(F32)
+                    * (dot_nt(values, mixed_grad[cols]) - inner[:, cols])
+                ).astype(BF16)
+                for cols in (slice(0, BALL), slice(BALL, 2 * BALL))
+            ],
+            axis=1,
+        )
+        values_grad = dot(weights, mixed_grad)
         keys_grad = dot(scores_grad, q_st[i, b])
         for n in range(LISTED):
             parts[b * LISTED + n, :, :OWN] = keys_grad[n * BALL : (n + 1) * BALL]
@@ -466,6 +490,7 @@
     near_gain[xy] = jnp.concatenate([gain_one_part, gain_two_part], axis=0)
     for copy in gain_first:
         copy.start()
+    loop(4, result_rows)
     sum_late.plane()
     for copy in gain_first:
         copy.wait()
@@ -553,8 +578,9 @@
             pltpu.VMEM((2, BALLS, BALL, 2 * OWN), BF16),
             pltpu.VMEM((2, BALLS, OWN, BALL), BF16),
             pltpu.VMEM((2, BALLS, OWN, BALL), BF16),
-            pltpu.VMEM((2, BALLS, LISTED * BALL, 2 * BALL), F32),
+            pltpu.VMEM((2, BALLS, LISTED * BALL, 2 * BALL), BF16),
             pltpu.VMEM((2, OWN, ROWS), BF16),
+            pltpu.VMEM((2, OWN, ROWS), F32),
             pltpu.VMEM((2, 2, ROWS, OWN), BF16),
             pltpu.VMEM((ROWS, 3 * OWN), BF16),
             pltpu.VMEM((LISTED * BALLS + 1, BALL, D), F32),
@@ -606,6 +632,7 @@
         out_shape=(rows, rows) + shapes + shapes,
         in_specs=[vmem()] * 5,
         out_specs=(vmem(),) * 8,
+        compiler_params=pltpu.CompilerParams(vmem_limit_bytes=16 << 20),
     )(early, late, gain_sums, result, points_grad)
 
 

time: 72 us -> 71.3 us (level)
  Pallas kernels: 71.3 us -> 65.7 us
  local copies, waits for them, and re-layouts: 0 us -> 4.66 us
    unnamed x0 -> x10, local copies, waits for them, and re-layouts: none -> 4.66 us
    pallas_call x1, Pallas kernels: 68.4 us -> 64.1 us  [layers_call(): pl.pallas_call(functools.partial(layers_kernel, near_count, planes), name...]
    pallas_call x1, Pallas kernels: 2.86 us -> 1.52 us  [spread_call(): pl.pallas_call(spread_kernel, name='spread', out_shape=(rows, rows) + sha...]
where the time goes in v4:
time: 71.3 us; the launch traced here: 71 us
  Pallas kernels  65.7 us (92%)
  local copies, waits for them, and re-layouts  4.66 us (7%)
    pallas_call x1, Pallas kernels, layers_call(): pl.pallas_call(functools.partial(layers_kernel, near_count, planes), name...  64.1 us
    unnamed x10, local copies, waits for them, and re-layouts  4.66 us
    pallas_call x1, Pallas kernels, spread_call(): pl.pallas_call(spread_kernel, name='spread', out_shape=(rows, rows) + sha...  1.52 us

profile of v4, /device:TPU:1, one launch (start us, length us, event | category | flops | bytes accessed | tf_op | source)
XLA Modules:
  0.0 71.0 jit_solution(10011379638055224752)
XLA Ops:
  0.6 64.1 %layers.1 = (bf16[1,512,256]{2,1,0:T(8,128)(2,1)}, bf16[1,512,256]{2,1,0:T(8,128)(2,1)}, bf16[2,256,640]{2,1,0:T(8,128)(2,1)}, bf16[2,256,384]{2,1,0:T(8,128)(2,1)}, f32[2,2,256]{2,1,0:T(2,128)}) custom-call(bf16[1,512,256]{2,1,0:T(8,128)(2,1)} %points.1, bf16[1,512,256]{2,1,0:T(8,128)(2,1)} %result_grad.1, s32[1,4,4]{2,1,0:T(4,128)} %lists_one.1, ...), custom_call_target="tpu_custom_call" | custom-call | tf_op jit(solution)/shard_map/layers/pallas_call | solution.py:556
  64.8 0.0 copy-start.4
  64.8 0.7 copy-done.4
  65.5 0.0 copy-start
  65.5 1.1 %copy-done = bf16[2,256,640]{2,1,0:T(8,128)(2,1)S(1)} copy-done((bf16[2,256,640]{2,1,0:T(8,128)(2,1)S(1)}, bf16[2,256,640]{2,1,0:T(8,128)(2,1)}, u32[]{:S(2)}) %copy-start) | copy-done | bytes 655384
  66.5 0.0 copy-start.1
  66.5 1.0 %copy-done.1 = bf16[2,256,384]{2,1,0:T(8,128)(2,1)S(1)} copy-done((bf16[2,256,384]{2,1,0:T(8,128)(2,1)S(1)}, bf16[2,256,384]{2,1,0:T(8,128)(2,1)}, u32[]{:S(2)}) %copy-start.1) | copy-done | bytes 393240
  67.5 0.0 copy-start.2
  67.5 0.9 %copy-done.2 = bf16[1,512,256]{2,1,0:T(8,128)(2,1)S(1)} copy-done((bf16[1,512,256]{2,1,0:T(8,128)(2,1)S(1)}, bf16[1,512,256]{2,1,0:T(8,128)(2,1)}, u32[]{:S(2)}) %copy-start.2) | copy-done | bytes 262168
  68.5 0.0 copy-start.3
  68.5 0.9 %copy-done.3 = bf16[1,512,256]{2,1,0:T(8,128)(2,1)S(1)} copy-done((bf16[1,512,256]{2,1,0:T(8,128)(2,1)S(1)}, bf16[1,512,256]{2,1,0:T(8,128)(2,1)}, u32[]{:S(2)}) %copy-start.3) | copy-done | bytes 262168
  69.4 1.5 %spread.1 = (bf16[1,512,256]{2,1,0:T(8,128)(2,1)}, bf16[1,512,256]{2,1,0:T(8,128)(2,1)}, f32[256]{0:T(256)}, f32[256,768]{1,0:T(8,128)}, f32[256,256]{1,0:T(8,12...) custom-call(bf16[2,256,640]{2,1,0:T(8,128)(2,1)S(1)} %copy-done, bf16[2,256,384]{2,1,0:T(8,128)(2,1)S(1)} %copy-done.1, ...), custom_call_target="tpu_custom_call" | custom-call | tf_op jit(solution)/shard_map/spread/pallas_call | solution.py:629
Async XLA Ops:
  64.8 0.7 copy-start.4
  65.5 1.1 %copy-start = (bf16[2,256,640]{2,1,0:T(8,128)(2,1)S(1)}, bf16[2,256,640]{2,1,0:T(8,128)(2,1)}, u32[]{:S(2)}) copy-start(bf16[2,256,640]{2,1,0:T(8,128)(2,1)} %get-tuple-element.13.early) | copy-start | bytes 1966084
  66.5 1.0 %copy-start.1 = (bf16[2,256,384]{2,1,0:T(8,128)(2,1)S(1)}, bf16[2,256,384]{2,1,0:T(8,128)(2,1)}, u32[]{:S(2)}) copy-start(bf16[2,256,384]{2,1,0:T(8,128)(2,1)} %get-tuple-element.14.late) | copy-start | bytes 1179652
  67.5 0.9 %copy-start.2 = (bf16[1,512,256]{2,1,0:T(8,128)(2,1)S(1)}, bf16[1,512,256]{2,1,0:T(8,128)(2,1)}, u32[]{:S(2)}) copy-start(bf16[1,512,256]{2,1,0:T(8,128)(2,1)} %get-tuple-element.16.result_in) | copy-start | bytes 786436
  68.5 0.9 %copy-start.3 = (bf16[1,512,256]{2,1,0:T(8,128)(2,1)S(1)}, bf16[1,512,256]{2,1,0:T(8,128)(2,1)}, u32[]{:S(2)}) copy-start(bf16[1,512,256]{2,1,0:T(8,128)(2,1)} %get-tuple-element.17.points_grad_in) | copy-start | bytes 786436

commit v5 on v4

--- a/solution.py
+++ b/solution.py
@@ -471,6 +471,7 @@
     loop(BALLS, lambda t: gather_parts(0, t))
     late[...] = dot(normed_t[0], dqkv[...]).astype(BF16)
     sum_late.scatter()
+    sum_early.plane()
 
     def partial_one(j):
         partial_rows(0, other * 4 + j)
@@ -478,7 +479,6 @@
 
     loop(4, partial_one)
     loop(4, lambda j: partial_rows(0, c * 4 + j))
-    sum_early.plane()
 
     def rows_one(j, total):
         ng_copy(0, other * 4 + j, j).wait()

time: 71.3 us -> 71.8 us (level)
  no operation moved by 1% of the time
where the time goes in v5:
time: 71.8 us; the launch traced here: 71.5 us
  Pallas kernels  66.2 us (92%)
  local copies, waits for them, and re-layouts  4.66 us (6%)
    pallas_call x1, Pallas kernels, layers_call(): pl.pallas_call(functools.partial(layers_kernel, near_count, planes), name...  64.7 us
    unnamed x10, local copies, waits for them, and re-layouts  4.66 us
    pallas_call x1, Pallas kernels, spread_call(): pl.pallas_call(spread_kernel, name='spread', out_shape=(rows, rows) + sha...  1.52 us

profile of v5, /device:TPU:1, one launch (start us, length us, event | category | flops | bytes accessed | tf_op | source)
XLA Modules:
  0.0 71.5 jit_solution(7786707438467721184)
XLA Ops:
  0.6 64.7 %layers.1 = (bf16[1,512,256]{2,1,0:T(8,128)(2,1)}, bf16[1,512,256]{2,1,0:T(8,128)(2,1)}, bf16[2,256,640]{2,1,0:T(8,128)(2,1)}, bf16[2,256,384]{2,1,0:T(8,128)(2,1)}, f32[2,2,256]{2,1,0:T(2,128)}) custom-call(bf16[1,512,256]{2,1,0:T(8,128)(2,1)} %points.1, bf16[1,512,256]{2,1,0:T(8,128)(2,1)} %result_grad.1, s32[1,4,4]{2,1,0:T(4,128)} %lists_one.1, ...), custom_call_target="tpu_custom_call" | custom-call | tf_op jit(solution)/shard_map/layers/pallas_call | solution.py:556
  65.3 0.0 copy-start.4
  65.3 0.7 copy-done.4
  66.0 0.0 copy-start
  66.0 1.1 %copy-done = bf16[2,256,640]{2,1,0:T(8,128)(2,1)S(1)} copy-done((bf16[2,256,640]{2,1,0:T(8,128)(2,1)S(1)}, bf16[2,256,640]{2,1,0:T(8,128)(2,1)}, u32[]{:S(2)}) %copy-start) | copy-done | bytes 655384
  67.1 0.0 copy-start.1
  67.1 1.0 %copy-done.1 = bf16[2,256,384]{2,1,0:T(8,128)(2,1)S(1)} copy-done((bf16[2,256,384]{2,1,0:T(8,128)(2,1)S(1)}, bf16[2,256,384]{2,1,0:T(8,128)(2,1)}, u32[]{:S(2)}) %copy-start.1) | copy-done | bytes 393240
  68.1 0.0 copy-start.2
  68.1 0.9 %copy-done.2 = bf16[1,512,256]{2,1,0:T(8,128)(2,1)S(1)} copy-done((bf16[1,512,256]{2,1,0:T(8,128)(2,1)S(1)}, bf16[1,512,256]{2,1,0:T(8,128)(2,1)}, u32[]{:S(2)}) %copy-start.2) | copy-done | bytes 262168
  69.0 0.0 copy-start.3
  69.0 0.9 %copy-done.3 = bf16[1,512,256]{2,1,0:T(8,128)(2,1)S(1)} copy-done((bf16[1,512,256]{2,1,0:T(8,128)(2,1)S(1)}, bf16[1,512,256]{2,1,0:T(8,128)(2,1)}, u32[]{:S(2)}) %copy-start.3) | copy-done | bytes 262168
  70.0 1.5 %spread.1 = (bf16[1,512,256]{2,1,0:T(8,128)(2,1)}, bf16[1,512,256]{2,1,0:T(8,128)(2,1)}, f32[256]{0:T(256)}, f32[256,768]{1,0:T(8,128)}, f32[256,256]{1,0:T(8,12...) custom-call(bf16[2,256,640]{2,1,0:T(8,128)(2,1)S(1)} %copy-done, bf16[2,256,384]{2,1,0:T(8,128)(2,1)S(1)} %copy-done.1, ...), custom_call_target="tpu_custom_call" | custom-call | tf_op jit(solution)/shard_map/spread/pallas_call | solution.py:629
Async XLA Ops:
  65.3 0.7 copy-start.4
  66.0 1.1 %copy-start = (bf16[2,256,640]{2,1,0:T(8,128)(2,1)S(1)}, bf16[2,256,640]{2,1,0:T(8,128)(2,1)}, u32[]{:S(2)}) copy-start(bf16[2,256,640]{2,1,0:T(8,128)(2,1)} %get-tuple-element.13.early) | copy-start | bytes 1966084
  67.1 1.0 %copy-start.1 = (bf16[2,256,384]{2,1,0:T(8,128)(2,1)S(1)}, bf16[2,256,384]{2,1,0:T(8,128)(2,1)}, u32[]{:S(2)}) copy-start(bf16[2,256,384]{2,1,0:T(8,128)(2,1)} %get-tuple-element.14.late) | copy-start | bytes 1179652
  68.1 0.9 %copy-start.2 = (bf16[1,512,256]{2,1,0:T(8,128)(2,1)S(1)}, bf16[1,512,256]{2,1,0:T(8,128)(2,1)}, u32[]{:S(2)}) copy-start(bf16[1,512,256]{2,1,0:T(8,128)(2,1)} %get-tuple-element.16.result_in) | copy-start | bytes 786436
  69.0 0.9 %copy-start.3 = (bf16[1,512,256]{2,1,0:T(8,128)(2,1)S(1)}, bf16[1,512,256]{2,1,0:T(8,128)(2,1)}, u32[]{:S(2)}) copy-start(bf16[1,512,256]{2,1,0:T(8,128)(2,1)} %get-tuple-element.17.points_grad_in) | copy-start | bytes 786436
